TPU v7x, 128 devices: a whole 4x4x4 slice. The times are simulated.
128 devices in a mesh: replica: 16 (over x_lo, z, core), tensor: 8 (over y, x_hi).
Axes of the slice: x: 4 (x_hi: 2, x_lo: 2; x = x_hi * 2 + x_lo), y: 4, z: 4, core: 2. Of those that a mesh axis runs over, the one named last changes fastest.
Arguments:
- tokens: bfloat16 [8192, 1024], P('replica'), may hold values from -6 to 6
- targets: bfloat16 [8192, 1024], P('replica'), may hold values from -6 to 6
- row_ids: int32 [16, 3, 512], P('replica'), may hold values from 0 to 511
- anchor: float32 [2, 1024, 4096], P(None, None, 'tensor'), may hold values from -0.1875 to 0.1875
- momentum: float32 [16, 2, 1024, 4096], P('replica', None, None, 'tensor'), may hold values from -4 to 4
- slow: float32 [2, 1024, 4096], P(None, None, 'tensor'), may hold values from -6 to 6
Outputs:
- anchor_new: float32 [2, 1024, 4096], P(None, None, 'tensor')
- slow_new: float32 [2, 1024, 4096], P(None, None, 'tensor')
- momentum_new: float32 [16, 2, 1024, 4096], P('replica', None, None, 'tensor')
Inputs may be any that keep to these rules, and one draw needn't show every extreme that they name: `row_ids`: each id names a row within its replica's own block of 512 rows; rows may repeat.
All inputs are finite; a program needn't handle non-finite values.
Results may differ from a plain program's by a relative error of at most 0.008.
Values may be sent and summed in bfloat16 or wider, within the bound.
A program may use at most 128 MiB of HBM per device.

v0:
```python
import jax
import jax.numpy as jnp
from jax import lax
from jax.sharding import PartitionSpec as P

INNER = 3


learn_rate = 0.02
inner_beta = 0.9
slow_beta = 0.5


def passed_along(block, axis, distance):
    devices = range(lax.axis_size(axis))
    route = [((i - distance) % len(devices), i) for i in devices]
    return lax.ppermute(block, axis, route)


def gelu_pair(pre):
    coeff = 0.7978845608028654
    inner = coeff * (pre + 0.044715 * pre * pre * pre)
    tanh_val = jnp.tanh(inner)
    value = 0.5 * pre * (1.0 + tanh_val)
    slope = 0.5 * (1.0 + tanh_val) + 0.5 * pre * (1.0 - tanh_val * tanh_val) * coeff * (
        1.0 + 3.0 * 0.044715 * pre * pre
    )
    return (value, slope)


def body(tokens, targets, row_ids, anchor, momentum, slow):
    row_count = tokens.shape[0]
    scale = 1.0 / row_count
    weights = anchor
    moment = momentum[0]
    for step in range(INNER):
        if step > 0:
            incoming = passed_along(weights.astype(jnp.bfloat16), "replica", 2 ** (step - 1))
            weights = 0.5 * (weights + incoming.astype(jnp.float32))
        picks = row_ids[0, step]
        inputs = jnp.take(tokens, picks, axis=0)
        wanted = jnp.take(targets, picks, axis=0)
        weights_bf = weights.astype(jnp.bfloat16)
        pre = jnp.dot(inputs, weights_bf[0], preferred_element_type=jnp.float32)
        value, slope = gelu_pair(pre)
        hidden = value.astype(jnp.bfloat16)
        partial_out = lax.dot_general(
            hidden, weights_bf[1], (((1,), (1,)), ((), ())), preferred_element_type=jnp.float32
        )
        summed = lax.psum(partial_out, "tensor")
        error = ((summed - wanted.astype(jnp.float32)) * scale).astype(jnp.bfloat16)
        back = (jnp.dot(error, weights_bf[1], preferred_element_type=jnp.float32) * slope).astype(
            jnp.bfloat16
        )
        grad_in = lax.dot_general(
            inputs, back, (((0,), (0,)), ((), ())), preferred_element_type=jnp.float32
        )
        grad_out = lax.dot_general(
            error, hidden, (((0,), (0,)), ((), ())), preferred_element_type=jnp.float32
        )
        moment = inner_beta * moment + jnp.stack([grad_in, grad_out])
        weights = weights - learn_rate * moment
    replicas = lax.axis_size("replica")
    total = lax.psum(weights, "replica")
    mean = total / replicas
    slow_new = slow_beta * slow + (anchor - mean) / learn_rate
    anchor_new = anchor - learn_rate * slow_new
    return (anchor_new, slow_new, moment[None])


def solution(mesh):
    return jax.shard_map(
        body,
        mesh=mesh,
        in_specs=(
            P("replica", None),
            P("replica", None),
            P("replica", None, None),
            P(None, None, "tensor"),
            P("replica", None, None, "tensor"),
            P(None, None, "tensor"),
        ),
        out_specs=(
            P(None, None, "tensor"),
            P(None, None, "tensor"),
            P("replica", None, None, "tensor"),
        ),
        check_vma=False,
    )
```

profile of v0, /device:TPU:1, one launch (start us, length us, event | category | flops | bytes accessed | tf_op | source)
XLA Modules:
  0.0 625.0 jit_solution(4985330071211238763)
XLA Ops:
  7.2 0.8 fusion.103
  8.0 3.8 convert_element_type.57
  11.8 2.0 gather_fusion
  13.9 2.1 fusion.34
  16.0 1.0 copy-done.19
  17.0 2.1 fusion.56
  19.2 1.1 copy-done.2
  20.4 2.8 gather_fusion.1
  23.1 105.7 %all-reduce.5.cloned.1.call-done = f32[512,1024]{1,0:T(8,128)} async-done(((f32[512,1024]{1,0:T(8,128)}), f32[512,1024]{1,0:T(8,128)}) %all-reduce.5.cloned.1.call-update) | async-done | bytes 2097168 | tf_op jit(solution)/shard_map/psum | solution.py:50
  128.8 5.6 fusion.13
  134.5 3.5 fusion.99
  137.9 1.8 copy-done.11
  139.7 0.8 copy-done.12
  140.5 4.5 fusion.83
  145.0 2.6 collective-permute-start
  147.6 2.1 gather_fusion.2
  149.7 21.2 %collective-permute-done = bf16[2,1024,512]{2,1,0:T(8,128)(2,1)} collective-permute-done((bf16[2,1024,512]{2,1,0:T(8,128)(2,1)}, bf16[2,1024,512]{2,1,0:T(8,128)(2,1)}, u32[]{:S(2)}, u32[]{:S(2)}) %collective-permute-start) | collective-permute-done | bytes 2097184 | tf_op jit(solution)/shard_map/ppermute | solution.py:17
  170.9 5.3 fusion.6
  176.3 0.8 fusion.33
  177.0 0.6 copy-done.16
  177.6 1.0 copy-done.20
  178.6 2.1 fusion.57
  181.0 2.8 gather_fusion.3
  183.8 102.4 %all-reduce.7.cloned.1.call-done = f32[512,1024]{1,0:T(8,128)} async-done(((f32[512,1024]{1,0:T(8,128)}), f32[512,1024]{1,0:T(8,128)}) %all-reduce.7.cloned.1.call-update) | async-done | bytes 2097168 | tf_op jit(solution)/shard_map/psum | solution.py:50
  286.2 5.6 fusion.12
  291.9 3.4 fusion.100
  295.3 1.8 copy-done.5
  297.2 0.8 copy-done.8
  297.9 5.1 fusion.102
  303.0 1.3 collective-permute-start.1
  304.3 2.1 gather_fusion.4
  306.4 44.8 %collective-permute-done.1 = bf16[2,1024,512]{2,1,0:T(8,128)(2,1)} collective-permute-done((bf16[2,1024,512]{2,1,0:T(8,128)(2,1)}, bf16[2,1024,512]{2,1,0:T(8,128)(2,1)}, u32[]{:S(2)}, u32[]{:S(2)}) %collective-permute-start.1) | collective-permute-done | bytes 2097184 | tf_op jit(solution)/shard_map/ppermute | solution.py:17
  351.2 3.6 fusion.7
  354.8 0.8 fusion.32
  355.5 0.6 copy-done.17
  356.1 2.2 fusion.58
  358.3 0.3 all-reduce.11.cloned.1.call-start
  358.6 2.1 gather_fusion.5
  360.7 102.3 %all-reduce.9.cloned.1.call-done = f32[512,1024]{1,0:T(8,128)} async-done(((f32[512,1024]{1,0:T(8,128)}), f32[512,1024]{1,0:T(8,128)}) %all-reduce.9.cloned.1.call-update) | async-done | bytes 2097168 | tf_op jit(solution)/shard_map/psum | solution.py:50
  462.9 5.4 fusion.11
  468.3 3.5 fusion.101
  471.8 1.3 copy-done.14
  473.1 0.5 copy-done.7
  473.6 0.8 copy-done.9
  474.4 5.4 fusion.1
  479.9 7.7 %fusion.5 = f32[1,2,1024,512]{3,2,1,0:T(8,128)} fusion(f32[1,1,1024,512]{3,2,1,0:T(8,128)} %bitcast.51, f32[1,1,1024,512]{3,2,1,0:T(8,128)} %bitcast.48, f32[1,1,1024,512]{3,2,1,0:T(8,128)} %bitcast.47, f32[1,1,1024,512]{3,2,1,0:T(8,128)S(1)} %bitcast.44, f32[1,1,1024,512]{3,2,1,0:T(8,128)} %bitcast.55, f32[1,1,1024,512]{3,2,1,0:T(8,128)} %bitcast.53, ...), kind=kLoop, calls=%fused_computation.15 | loop fusion | flops 9437184 | bytes 20971520 | tf_op jit(solution)/shard_map/add | solution.py:61
  487.5 120.7 %all-reduce.11.cloned.1.call-done = f32[2,1024,512]{2,1,0:T(8,128)} async-done(((f32[2,1024,512]{2,1,0:T(8,128)}), f32[2,1024,512]{2,1,0:T(8,128)}) %all-reduce.11.cloned.1.call-update) | async-done | bytes 4194320 | tf_op jit(solution)/shard_map/psum | solution.py:64
  608.2 10.2 %multiply_subtract_fusion = (f32[2,1024,512]{2,1,0:T(8,128)}, f32[2,1024,512]{2,1,0:T(8,128)}) fusion(f32[2,1024,512]{2,1,0:T(8,128)} %param.11, f32[2,1024,512]{2,1,0:T(8,128)} %all-reduce.11.cloned.1.call-done, f32[2,1024,512]{2,1,0:T(8,128)} %param.13), kind=kLoop, calls=%fused_computation.16 | loop fusion | flops 7340032 | bytes 20971520 | tf_op jit(solution)/shard_map/sub | solution.py:67
  (48 shorter events, 0.5 us)
Async XLA Ops:
  7.2 4.7 copy-start
  7.2 121.7 %all-reduce.5.cloned.1.call-start = ((), (), s32[]{:S(2)}) async-start(), calls=%async_computation | async-start | bytes 4194304 | tf_op jit(solution)/shard_map/psum | solution.py:50
  13.9 3.1 copy-start.15
  16.0 1.0 copy-start.19
  19.1 1.2 copy-start.2
  19.2 267.0 %all-reduce.7.cloned.1.call-start = ((), (), s32[]{:S(2)}) async-start(), calls=%async_computation.1 | async-start | bytes 4194304 | tf_op jit(solution)/shard_map/psum | solution.py:50
  134.4 3.5 copy-start.3
  134.4 5.3 copy-start.11
  134.4 6.1 copy-start.12
  137.9 7.1 %copy-start.13 = (f32[1024,512]{1,0:T(8,128)}, f32[1024,512]{1,0:T(8,128)S(1)}, u32[]{:S(2)}) copy-start(f32[1024,512]{1,0:T(8,128)S(1)} %fusion.99) | copy-start | bytes 6291460
  145.0 25.9 %collective-permute-start = (bf16[2,1024,512]{2,1,0:T(8,128)(2,1)}, bf16[2,1024,512]{2,1,0:T(8,128)(2,1)}, u32[]{:S(2)}, u32[]{:S(2)}) collective-permute-start(bf16[2,1024,512]{2,1,0:T(8,128)(2,1)} %get-tuple-element.8), channel_id=1, source_target_pairs={{120,0},{0,8},{8,16},{16,24},{24,32},{32,40},{40,48},{48,56},{56,6... | collective-permute-start | bytes 6291464 | tf_op jit(solution)/shard_map/ppermute | solution.py:17
  176.2 1.4 copy-start.16
  177.6 1.0 copy-start.20
  180.7 282.2 %all-reduce.9.cloned.1.call-start = ((), (), s32[]{:S(2)}) async-start(), calls=%async_computation.2 | async-start | bytes 4194304 | tf_op jit(solution)/shard_map/psum | solution.py:50
  291.9 3.5 copy-start.4
  291.9 5.3 copy-start.5
  291.9 6.1 copy-start.8
  295.3 7.7 %copy-start.10 = (f32[1024,512]{1,0:T(8,128)}, f32[1024,512]{1,0:T(8,128)S(1)}, u32[]{:S(2)}) copy-start(f32[1024,512]{1,0:T(8,128)S(1)} %fusion.100) | copy-start | bytes 6291460
  303.0 48.2 %collective-permute-start.1 = (bf16[2,1024,512]{2,1,0:T(8,128)(2,1)}, bf16[2,1024,512]{2,1,0:T(8,128)(2,1)}, u32[]{:S(2)}, u32[]{:S(2)}) collective-permute-start(bf16[2,1024,512]{2,1,0:T(8,128)(2,1)} %get-tuple-element.6), channel_id=1, source_target_pairs={{112,0},{120,8},{0,16},{8,24},{16,32},{24,40},{32,48},{40,56},{48,... | collective-permute-start | bytes 6291464 | tf_op jit(solution)/shard_map/ppermute | solution.py:17
  354.8 1.3 copy-start.17
  356.1 2.2 copy-start.21
  358.3 249.9 %all-reduce.11.cloned.1.call-start = ((), (), s32[]{:S(2)}) async-start(), calls=%async_computation.3 | async-start | bytes 8388608 | tf_op jit(solution)/shard_map/psum | solution.py:64
  360.7 102.3 %copy-start.18 = (bf16[512,1024]{1,0:T(8,128)(2,1)}, bf16[512,1024]{1,0:T(8,128)(2,1)S(1)}, u32[]{:S(2)}) copy-start(bf16[512,1024]{1,0:T(8,128)(2,1)S(1)} %gather_fusion.5) | copy-start | bytes 3145732
  468.3 4.8 copy-start.6
  468.3 5.3 copy-start.7
  468.3 6.1 copy-start.9
  471.8 1.3 copy-start.14
  608.2 10.2 %copy-start.1 = (bf16[512,1024]{1,0:T(8,128)(2,1)S(1)}, bf16[512,1024]{1,0:T(8,128)(2,1)}, u32[]{:S(2)}) copy-start(bf16[512,1024]{1,0:T(8,128)(2,1)} %param.8) | copy-start | bytes 3145732
Sparse Core Ops, SparseCore 0:
  19.3 109.5 all-reduce.4
  180.9 105.3 all-reduce.6
  358.4 104.4 all-reduce.8
  480.0 128.1 all-reduce.10
where the time goes:
time: 625 us
  waiting for transfers between devices  497 us (80%)
  other arithmetic  45.6 us (7%)
  matrix products  37 us (6%)
  local copies, waits for them, and re-layouts  26.7 us (4%)
  between operations  14 us (2%)
    psum x3, waiting for transfers between devices, body(): summed = lax.psum(partial_out, 'tensor')  310 us
    psum x1, waiting for transfers between devices, body(): total = lax.psum(weights, 'replica')  121 us
    ppermute x2, waiting for transfers between devices, passed_along(): return lax.ppermute(block, axis, route)  66 us
    dot_general x3, matrix products, body(): lax.dot_general(inputs, back, (((0,), (0,)), ((), ())), preferred_element...  16.7 us
    convert_element_type x3, other arithmetic, body(): weights_bf = weights.astype(jnp.bfloat16)  12.7 us
  transfers between devices with their start and end apart: 6, of which 6 were waited for; matrix products, arithmetic and copies ran while one was open for 3% of the time, Pallas kernels for 0%

commit v1 on v0

--- a/solution.py
+++ b/solution.py
@@ -33,22 +33,27 @@
     scale = 1.0 / row_count
     weights = anchor
     moment = momentum[0]
+    parts = lax.axis_size("tensor")
+    own = lax.axis_index("tensor")
+    shard_rows = row_count // parts
     for step in range(INNER):
         if step > 0:
             incoming = passed_along(weights.astype(jnp.bfloat16), "replica", 2 ** (step - 1))
             weights = 0.5 * (weights + incoming.astype(jnp.float32))
         picks = row_ids[0, step]
         inputs = jnp.take(tokens, picks, axis=0)
-        wanted = jnp.take(targets, picks, axis=0)
+        own_picks = lax.dynamic_slice(picks, (own * shard_rows,), (shard_rows,))
+        wanted = jnp.take(targets, own_picks, axis=0)
         weights_bf = weights.astype(jnp.bfloat16)
         pre = jnp.dot(inputs, weights_bf[0], preferred_element_type=jnp.float32)
         value, slope = gelu_pair(pre)
         hidden = value.astype(jnp.bfloat16)
         partial_out = lax.dot_general(
             hidden, weights_bf[1], (((1,), (1,)), ((), ())), preferred_element_type=jnp.float32
-        )
-        summed = lax.psum(partial_out, "tensor")
-        error = ((summed - wanted.astype(jnp.float32)) * scale).astype(jnp.bfloat16)
+        ).astype(jnp.bfloat16)
+        summed = lax.psum_scatter(partial_out, "tensor", scatter_dimension=0, tiled=True)
+        error = ((summed.astype(jnp.float32) - wanted.astype(jnp.float32)) * scale).astype(jnp.bfloat16)
+        error = lax.all_gather(error, "tensor", axis=0, tiled=True)
         back = (jnp.dot(error, weights_bf[1], preferred_element_type=jnp.float32) * slope).astype(
             jnp.bfloat16
         )
@@ -61,9 +66,10 @@
         moment = inner_beta * moment + jnp.stack([grad_in, grad_out])
         weights = weights - learn_rate * moment
     replicas = lax.axis_size("replica")
-    total = lax.psum(weights, "replica")
-    mean = total / replicas
-    slow_new = slow_beta * slow + (anchor - mean) / learn_rate
+    moved = ((anchor - weights) / learn_rate).astype(jnp.bfloat16)
+    total = lax.psum_scatter(moved, "replica", scatter_dimension=1, tiled=True)
+    total = lax.all_gather(total, "replica", axis=1, tiled=True)
+    slow_new = slow_beta * slow + total.astype(jnp.float32) / replicas
     anchor_new = anchor - learn_rate * slow_new
     return (anchor_new, slow_new, moment[None])
 

time: 625 us -> 629 us (level)
  other arithmetic: 45.6 us -> 55.4 us
  local copies, waits for them, and re-layouts: 26.7 us -> 17.4 us
  waiting for transfers between devices: 497 us -> 505 us
    psum x4 -> x0, waiting for transfers between devices: 431 us -> none  [the longest x3 310 us: body(): summed = lax.psum(partial_out, 'tensor')]
    reduce_scatter x0 -> x4, waiting for transfers between devices: none -> 271 us  [the longest x3 210 us: body(): lax.psum_scatter(partial_out, 'tensor', scatter_dimension=0, tiled=True)]
    all_gather x0 -> x4, waiting for transfers between devices: none -> 170 us  [the longest x3 139 us: body(): error = lax.all_gather(error, 'tensor', axis=0, tiled=True)]
    convert_element_type x0 -> x4, other arithmetic: none -> 11.9 us  [the longest x1 6.9 us: body(): moved = ((anchor - weights) / learn_rate).astype(jnp.bfloat16)]
  transfers between devices with their start and end apart: 6 -> 10, of which waited for: 6 -> 10; matrix products, arithmetic and copies ran while one was open for 3% -> 2% of each run, Pallas kernels for 0% -> 0%
where the time goes in v1:
time: 629 us; the launch traced here: 628 us
  waiting for transfers between devices  505 us (80%)
  other arithmetic  55.4 us (9%)
  matrix products  31.2 us (5%)
  local copies, waits for them, and re-layouts  17.4 us (3%)
  between operations  14.4 us (2%)
    reduce_scatter x3, waiting for transfers between devices, body(): lax.psum_scatter(partial_out, 'tensor', scatter_dimension=0, tiled=True)  210 us
    all_gather x3, waiting for transfers between devices, body(): error = lax.all_gather(error, 'tensor', axis=0, tiled=True)  139 us
    ppermute x2, waiting for transfers between devices, passed_along(): return lax.ppermute(block, axis, route)  63.7 us
    reduce_scatter x1, waiting for transfers between devices, body(): total = lax.psum_scatter(moved, 'replica', scatter_dimension=1, tiled=True)  60.7 us
    all_gather x1, waiting for transfers between devices, body(): total = lax.all_gather(total, 'replica', axis=1, tiled=True)  30.7 us
    convert_element_type x3, other arithmetic, body(): weights_bf = weights.astype(jnp.bfloat16)  14.2 us
    dot_general x3, matrix products, body(): lax.dot_general(inputs, back, (((0,), (0,)), ((), ())), preferred_element...  13.1 us
  transfers between devices with their start and end apart: 10, of which 10 were waited for; matrix products, arithmetic and copies ran while one was open for 2% of the time, Pallas kernels for 0%

profile of v1, /device:TPU:1, one launch (start us, length us, event | category | flops | bytes accessed | tf_op | source)
XLA Modules:
  0.0 628.3 jit_solution(16959371402139294303)
XLA Ops:
  7.2 0.8 fusion.106
  8.1 2.5 convert_element_type.81
  10.5 2.8 gather_fusion
  13.3 2.0 fusion.37
  15.3 1.0 copy-done.19
  16.3 3.1 convolution_convert_fusion.2
  19.6 0.7 gather_fusion.1
  20.3 72.9 %reduce-scatter.5.cloned.1.call-done = bf16[64,1024]{1,0:T(8,128)(2,1)} async-done(((bf16[512,1024]{1,0:T(8,128)(2,1)}), bf16[64,1024]{1,0:T(8,128)(2,1)}) %reduce-scatter.5.cloned.1.call-update) | async-done | bytes 131088 | tf_op jit(solution)/shard_map/reduce_scatter | solution.py:54
  93.2 1.7 multiply_convert_fusion.5
  95.0 46.8 %all-gather.5.cloned.1.call-done = bf16[512,1024]{1,0:T(8,128)(2,1)} async-done(((bf16[64,1024]{1,0:T(8,128)(2,1)}), bf16[512,1024]{1,0:T(8,128)(2,1)}) %all-gather.5.cloned.1.call-update) | async-done | bytes 1048592 | tf_op jit(solution)/shard_map/all_gather | solution.py:56
  141.8 3.9 fusion.16
  145.7 3.2 fusion.102
  149.2 7.0 %fusion.86 = (bf16[2,1024,512]{2,1,0:T(8,128)(2,1)}, f32[2,1024,512]{2,1,0:T(8,128)}) fusion(f32[2,1024,512]{2,1,0:T(8,128)S(1)} %copy-done.2, f32[1,1024,512]{2,1,0:T(8,128)S(1)} %bitcast.73, f32[1,1024,512]{2,1,0:T(8,128)S(1)} %bitcast.71, f32[1,2,1024,512]{3,2,1,0:T(8,128)} %param.14), kind=kLoop, calls=%fused_computation.144 | loop fusion | flops 6291456 | bytes 18874368 | tf_op jit(solution)/shard_map/convert_element_type | solution.py:41
  156.2 3.4 collective-permute-start
  159.7 2.8 gather_fusion.2
  162.5 20.5 %collective-permute-done = bf16[2,1024,512]{2,1,0:T(8,128)(2,1)S(1)} collective-permute-done((bf16[2,1024,512]{2,1,0:T(8,128)(2,1)}, bf16[2,1024,512]{2,1,0:T(8,128)(2,1)S(1)}, u32[]{:S(2)}, u32[]{:S(2)}) %collective-permute-start) | collective-permute-done | bytes 2097184 | tf_op jit(solution)/shard_map/ppermute | solution.py:17
  183.0 5.5 fusion.9
  188.5 0.8 fusion.36
  189.3 0.6 copy-done.15
  189.8 1.0 copy-done.21
  190.8 1.8 convolution_convert_fusion.1
  192.8 0.7 gather_fusion.3
  193.5 69.1 %reduce-scatter.7.cloned.1.call-done = bf16[64,1024]{1,0:T(8,128)(2,1)} async-done(((bf16[512,1024]{1,0:T(8,128)(2,1)}), bf16[64,1024]{1,0:T(8,128)(2,1)}) %reduce-scatter.7.cloned.1.call-update) | async-done | bytes 131088 | tf_op jit(solution)/shard_map/reduce_scatter | solution.py:54
  262.5 1.7 multiply_convert_fusion.4
  264.5 45.9 %all-gather.7.cloned.1.call-done = bf16[512,1024]{1,0:T(8,128)(2,1)} async-done(((bf16[64,1024]{1,0:T(8,128)(2,1)}), bf16[512,1024]{1,0:T(8,128)(2,1)}) %all-gather.7.cloned.1.call-update) | async-done | bytes 1048592 | tf_op jit(solution)/shard_map/all_gather | solution.py:56
  310.4 3.9 fusion.15
  314.3 2.5 fusion.103
  317.1 5.2 fusion.105
  322.3 1.3 collective-permute-start.1
  323.6 2.8 gather_fusion.4
  326.4 43.2 %collective-permute-done.1 = bf16[2,1024,512]{2,1,0:T(8,128)(2,1)} collective-permute-done((bf16[2,1024,512]{2,1,0:T(8,128)(2,1)}, bf16[2,1024,512]{2,1,0:T(8,128)(2,1)}, u32[]{:S(2)}, u32[]{:S(2)}) %collective-permute-start.1) | collective-permute-done | bytes 2097184 | tf_op jit(solution)/shard_map/ppermute | solution.py:17
  369.7 6.3 %fusion.10 = bf16[2,1024,512]{2,1,0:T(8,128)(2,1)S(1)} fusion(bf16[2,1024,512]{2,1,0:T(8,128)(2,1)} %collective-permute-done.1, f32[1,1024,512]{2,1,0:T(8,128)} %bitcast.68, f32[1,1024,512]{2,1,0:T(8,128)S(1)} %bitcast.64, f32[2,1024,512]{2,1,0:T(8,128)} %get-tuple-element.12, bf16[2,1024,512]{2,1,0:T(8,128)(2,1)} %copy-done.6, f32[2,1024,512]{2,1,0:T(8,128)} %param.13), kind=kLoop, calls=%fused_computation.26 | loop fusion | flops 14680064 | bytes 18874368 | tf_op jit(solution)/shard_map/convert_element_type | solution.py:47
  376.0 0.8 fusion.35
  376.7 0.6 copy-done.14
  377.3 1.0 copy-done.20
  378.3 1.8 convolution_convert_fusion
  380.2 0.7 gather_fusion.5
  380.9 68.4 %reduce-scatter.9.cloned.1.call-done = bf16[64,1024]{1,0:T(8,128)(2,1)} async-done(((bf16[512,1024]{1,0:T(8,128)(2,1)}), bf16[64,1024]{1,0:T(8,128)(2,1)}) %reduce-scatter.9.cloned.1.call-update) | async-done | bytes 131088 | tf_op jit(solution)/shard_map/reduce_scatter | solution.py:54
  449.3 1.7 multiply_convert_fusion.3
  451.1 46.2 %all-gather.9.cloned.1.call-done = bf16[512,1024]{1,0:T(8,128)(2,1)} async-done(((bf16[64,1024]{1,0:T(8,128)(2,1)}), bf16[512,1024]{1,0:T(8,128)(2,1)}) %all-gather.9.cloned.1.call-update) | async-done | bytes 1048592 | tf_op jit(solution)/shard_map/all_gather | solution.py:56
  497.3 5.3 fusion.14
  502.6 2.2 fusion.104
  504.9 1.3 copy-done.12
  506.2 6.9 %fusion.4 = bf16[2,1024,512]{2,1,0:T(8,128)(2,1)} fusion(f32[2,1024,512]{2,1,0:T(8,128)S(1)} %copy-done.4, f32[1,1024,512]{2,1,0:T(8,128)S(1)} %bitcast.77, f32[1,1024,512]{2,1,0:T(8,128)} %bitcast.75, bf16[2,1024,512]{2,1,0:T(8,128)(2,1)} %collective-permute-done.1, f32[1,1024,512]{2,1,0:T(8,128)} %bitcast.69, f32[1,1024,512]{2,1,0:T(8,128)S(1)} %bitcast.65, ...), kind=kLoop, calls=%fused_computation.13 | loop fusion | flops 22020096 | bytes 23068672 | tf_op jit(solution)/shard_map/convert_element_type | solution.py:69
  513.4 60.7 %reduce-scatter.11.cloned.1.call-done = bf16[2,64,512]{2,1,0:T(8,128)(2,1)} async-done(((bf16[2,1024,512]{2,1,0:T(8,128)(2,1)}), bf16[2,64,512]{2,1,0:T(8,128)(2,1)}) %reduce-scatter.11.cloned.1.call-update) | async-done | bytes 131088 | tf_op jit(solution)/shard_map/reduce_scatter | solution.py:70
  574.1 7.7 %fusion.8 = f32[1,2,1024,512]{3,2,1,0:T(8,128)} fusion(f32[1,1,1024,512]{3,2,1,0:T(8,128)} %bitcast.74, f32[1,1,1024,512]{3,2,1,0:T(8,128)} %bitcast.72, f32[1,1,1024,512]{3,2,1,0:T(8,128)} %bitcast.70, f32[1,1,1024,512]{3,2,1,0:T(8,128)S(1)} %bitcast.66, f32[1,1,1024,512]{3,2,1,0:T(8,128)} %bitcast.78, f32[1,1,1024,512]{3,2,1,0:T(8,128)} %bitcast.76, ...), kind=kLoop, calls=%fused_computation.18 | loop fusion | flops 9437184 | bytes 20971520 | tf_op jit(solution)/shard_map/add | solution.py:66
  581.8 30.7 %all-gather.11.cloned.1.call-done = bf16[2,1024,512]{2,1,0:T(8,128)(2,1)} async-done(((bf16[2,64,512]{2,1,0:T(8,128)(2,1)}), bf16[2,1024,512]{2,1,0:T(8,128)(2,1)}) %all-gather.11.cloned.1.call-update) | async-done | bytes 2097168 | tf_op jit(solution)/shard_map/all_gather | solution.py:71
  612.5 9.0 %multiply_subtract_fusion = (f32[2,1024,512]{2,1,0:T(8,128)}, f32[2,1024,512]{2,1,0:T(8,128)}) fusion(f32[2,1024,512]{2,1,0:T(8,128)} %param.13, bf16[2,1024,512]{2,1,0:T(8,128)(2,1)} %all-gather.11.cloned.1.call-done, f32[2,1024,512]{2,1,0:T(8,128)} %param.15), kind=kLoop, calls=%fused_computation.19 | loop fusion | flops 6291456 | bytes 18874368 | tf_op jit(solution)/shard_map/sub | solution.py:73
  (69 shorter events, 1.9 us)
Async XLA Ops:
  7.2 3.4 copy-start
  7.2 86.0 %reduce-scatter.5.cloned.1.call-start = ((), (), s32[]{:S(2)}) async-start(), calls=%async_computation.4 | async-start | bytes 1179648 | tf_op jit(solution)/shard_map/reduce_scatter | solution.py:54
  10.5 2.8 copy-start.13
  15.3 1.0 copy-start.19
  16.3 3.3 copy-start.7
  19.4 122.3 %all-gather.5.cloned.1.call-start = ((), (), s32[]{:S(2)}) async-start(), calls=%async_computation.5 | async-start | bytes 1179648 | tf_op jit(solution)/shard_map/all_gather | solution.py:56
  94.9 167.6 %reduce-scatter.7.cloned.1.call-start = ((), (), s32[]{:S(2)}) async-start(), calls=%async_computation.6 | async-start | bytes 1179648 | tf_op jit(solution)/shard_map/reduce_scatter | solution.py:54
  145.7 10.6 %copy-start.10 = (f32[1024,512]{1,0:T(8,128)}, f32[1024,512]{1,0:T(8,128)S(1)}, u32[]{:S(2)}) copy-start(f32[1024,512]{1,0:T(8,128)S(1)} %fusion.16) | copy-start | bytes 6291460
  145.7 3.6 copy-start.2
  148.9 7.3 %copy-start.11 = (f32[1024,512]{1,0:T(8,128)}, f32[1024,512]{1,0:T(8,128)S(1)}, u32[]{:S(2)}) copy-start(f32[1024,512]{1,0:T(8,128)S(1)} %fusion.102) | copy-start | bytes 6291460
  156.2 26.7 %collective-permute-start = (bf16[2,1024,512]{2,1,0:T(8,128)(2,1)}, bf16[2,1024,512]{2,1,0:T(8,128)(2,1)S(1)}, u32[]{:S(2)}, u32[]{:S(2)}) collective-permute-start(bf16[2,1024,512]{2,1,0:T(8,128)(2,1)} %get-tuple-element.11), channel_id=1, source_target_pairs={{120,0},{0,8},{8,16},{16,24},{24,32},{32,40},{40,48},{48,56},{56,6... | collective-permute-start | bytes 6291464 | tf_op jit(solution)/shard_map/ppermute | solution.py:17
  183.0 5.5 copy-start.6
  183.0 5.5 copy-start.16
  188.5 1.3 copy-start.15
  189.8 1.0 copy-start.21
  190.8 1.9 copy-start.8
  192.6 117.8 %all-gather.7.cloned.1.call-start = ((), (), s32[]{:S(2)}) async-start(), calls=%async_computation.7 | async-start | bytes 1179648 | tf_op jit(solution)/shard_map/all_gather | solution.py:56
  264.2 185.1 %reduce-scatter.9.cloned.1.call-start = ((), (), s32[]{:S(2)}) async-start(), calls=%async_computation.8 | async-start | bytes 1179648 | tf_op jit(solution)/shard_map/reduce_scatter | solution.py:54
  314.3 2.8 copy-start.3
  316.9 5.4 copy-start.5
  322.3 47.3 %collective-permute-start.1 = (bf16[2,1024,512]{2,1,0:T(8,128)(2,1)}, bf16[2,1024,512]{2,1,0:T(8,128)(2,1)}, u32[]{:S(2)}, u32[]{:S(2)}) collective-permute-start(bf16[2,1024,512]{2,1,0:T(8,128)(2,1)} %fusion.105), channel_id=1, source_target_pairs={{112,0},{120,8},{0,16},{8,24},{16,32},{24,40},{32,48},{40,56},{48,... | collective-permute-start | bytes 6291464 | tf_op jit(solution)/shard_map/ppermute | solution.py:17
  326.4 49.5 %copy-start.17 = (bf16[512,1024]{1,0:T(8,128)(2,1)S(1)}, bf16[512,1024]{1,0:T(8,128)(2,1)}, u32[]{:S(2)}) copy-start(bf16[512,1024]{1,0:T(8,128)(2,1)} %gather_fusion.4) | copy-start | bytes 3145732
  376.0 1.3 copy-start.14
  377.3 1.0 copy-start.20
  378.3 1.9 copy-start.9
  380.1 117.2 %all-gather.9.cloned.1.call-start = ((), (), s32[]{:S(2)}) async-start(), calls=%async_computation.9 | async-start | bytes 1179648 | tf_op jit(solution)/shard_map/all_gather | solution.py:56
  451.0 123.1 %reduce-scatter.11.cloned.1.call-start = ((), (), s32[]{:S(2)}) async-start(), calls=%async_computation.10 | async-start | bytes 2228224 | tf_op jit(solution)/shard_map/reduce_scatter | solution.py:70
  497.2 5.3 copy-start.18
  502.6 3.6 copy-start.4
  504.8 1.3 copy-start.12
  513.1 99.4 %all-gather.11.cloned.1.call-start = ((), (), s32[]{:S(2)}) async-start(), calls=%async_computation.11 | async-start | bytes 2228224 | tf_op jit(solution)/shard_map/all_gather | solution.py:71
  612.5 9.0 %copy-start.1 = (bf16[512,1024]{1,0:T(8,128)(2,1)S(1)}, bf16[512,1024]{1,0:T(8,128)(2,1)}, u32[]{:S(2)}) copy-start(bf16[512,1024]{1,0:T(8,128)(2,1)} %param.10) | copy-start | bytes 3145732
Sparse Core Ops, SparseCore 0:
  19.5 73.6 reduce-scatter.4
  96.1 45.5 all-gather.4
  192.7 69.7 reduce-scatter.6
  264.8 45.6 all-gather.6
  380.2 69.1 reduce-scatter.8
  451.6 45.6 all-gather.8
  513.2 60.8 reduce-scatter.10
  575.8 36.6 all-gather.10

commit v2 on v0

v2 whole, which is shorter than its diff:
```python
import functools

import jax
import jax.numpy as jnp
from jax import lax
from jax.experimental import pallas as pl
from jax.experimental.pallas import tpu as pltpu
from jax.sharding import PartitionSpec as P

INNER = 3
learn_rate = 0.02
inner_beta = 0.9
slow_beta = 0.5

F32 = jnp.float32
BF16 = jnp.bfloat16
MESH = pl.DeviceIdType.MESH


def gelu_pair(pre):
    coeff = 0.7978845608028654
    square = pre * pre
    tanh_val = jnp.tanh(coeff * (pre + 0.044715 * pre * square))
    upper = 0.5 * (1.0 + tanh_val)
    value = pre * upper
    slope = upper + 0.5 * pre * (1.0 - tanh_val * tanh_val) * coeff * (
        1.0 + 3.0 * 0.044715 * square
    )
    return (value, slope)


def contract(a, b, dim_a, dim_b):
    return lax.dot_general(a, b, (((dim_a,), (dim_b,)), ((), ())), preferred_element_type=F32)


class Exchange:
    def __init__(self, pos, half, up, down, pair, block, part, hop, mid, fin, give, got, full, send, recv):
        self.pos, self.half, self.up, self.down, self.pair = pos, half, up, down, pair
        self.block, self.part, self.hop, self.mid, self.fin = block, part, hop, mid, fin
        self.give, self.got, self.full, self.send, self.recv = give, got, full, send, recv
        self.sent = []

    def copy(self, src, dst, index, device):
        return pltpu.make_async_remote_copy(
            src_ref=src,
            dst_ref=dst,
            send_sem=self.send.at[index],
            recv_sem=self.recv.at[index],
            device_id=device,
            device_id_type=MESH,
        )

    def start(self, src, dst, index, device):
        copy = self.copy(src, dst, index, device)
        copy.start()
        self.sent.append(copy)
        return copy

    def piece(self, chunk, half):
        return self.part.at[chunk, half]

    def reduce(self, make):
        pos = self.pos
        far, above, below = (pos + 2) % 4, (pos + 1) % 4, (pos + 3) % 4
        make(far)
        first_up = self.start(self.piece(far, 0), self.hop.at[0], 0, self.up)
        first_down = self.start(self.piece(far, 1), self.hop.at[1], 1, self.down)
        make(above)
        self.start(self.piece(above, 1), self.fin.at[1, 0], 2, self.up)
        make(below)
        self.start(self.piece(below, 0), self.fin.at[0, 0], 3, self.down)
        first_up.wait_recv()
        self.mid[0] = (self.part[above, 0].astype(F32) + self.hop[0].astype(F32)).astype(BF16)
        self.start(self.mid.at[0], self.fin.at[0, 1], 4, self.up)
        first_down.wait_recv()
        self.mid[1] = (self.part[below, 1].astype(F32) + self.hop[1].astype(F32)).astype(BF16)
        self.start(self.mid.at[1], self.fin.at[1, 1], 5, self.down)
        make(pos)
        for copy in self.sent[2:6]:
            copy.wait_recv()
        self.give[...] = self.total(1 - self.half).astype(BF16)
        last = self.start(self.give, self.got, 6, self.pair)
        mine = self.total(self.half)
        last.wait_recv()
        return mine + self.got[...].astype(F32)

    def total(self, half):
        return (
            self.part[self.pos, half].astype(F32)
            + self.fin[half, 0].astype(F32)
            + self.fin[half, 1].astype(F32)
        )

    def slot(self, chunk, half):
        return self.full.at[pl.ds(pl.multiple_of((chunk * 2 + half) * self.block, self.block), self.block)]

    def gather(self, arrived):
        pos, half = self.pos, self.half
        far, above, below = (pos + 2) % 4, (pos + 1) % 4, (pos + 3) % 4
        own, other = self.slot(pos, half), self.slot(pos, 1 - half)
        self.start(own, own, 7, self.pair)
        self.start(own, own, 8, self.up)
        self.start(own, own, 9, self.down)
        self.copy(other, other, 7, self.pair).wait_recv()
        self.start(other, other, 10, self.up)
        self.start(other, other, 11, self.down)
        arrived(pos)
        self.copy(own, self.slot(below, half), 8, self.up).wait_recv()
        self.copy(own, self.slot(above, half), 9, self.down).wait_recv()
        self.copy(own, self.slot(below, 1 - half), 10, self.up).wait_recv()
        self.copy(own, self.slot(above, 1 - half), 11, self.down).wait_recv()
        low, high = self.slot(below, 0), self.slot(above, 1)
        self.start(low, low, 12, self.up)
        self.start(high, high, 13, self.down)
        arrived(below)
        arrived(above)
        self.copy(own, self.slot(far, 0), 12, self.up).wait_recv()
        self.copy(own, self.slot(far, 1), 13, self.down).wait_recv()
        arrived(far)

    def finish(self):
        for copy in self.sent:
            copy.wait_send()


def kernel(
    ids, tokens, targets, anchor, momentum,
    moment_out, total_out,
    weights, moment, gone, cast, out_box, in_box, inputs, hidden, slope, back,
    part, hop, mid, fin, give, got, error,
    part2, hop2, mid2, fin2, give2, got2, total,
    send, recv, send2, recv2, box_send, box_recv, core_send, core_recv, local,
):
    rep, ten = lax.axis_index("replica"), lax.axis_index("tensor")
    row, side = ten // 2, ten % 2
    low, depth, core = rep // 8, (rep // 2) % 4, rep % 2
    up, down = (rep, (row + 1) % 4 * 2 + side), (rep, (row + 3) % 4 * 2 + side)
    pair = (rep, row * 2 + 1 - side)
    up2 = (low * 8 + (depth + 1) % 4 * 2 + core, ten)
    down2 = (low * 8 + (depth + 3) % 4 * 2 + core, ten)
    pair2 = ((1 - low) * 8 + depth * 2 + core, ten)
    twin = (low * 8 + depth * 2 + 1 - core, ten)

    load = [
        pltpu.make_async_copy(anchor.at[0], weights.at[0], local.at[0]),
        pltpu.make_async_copy(anchor.at[1], weights.at[1], local.at[1]),
        pltpu.make_async_copy(momentum.at[0], moment, local.at[2]),
    ]
    for copy in load:
        copy.start()

    barrier = pltpu.get_barrier_semaphore()
    peers = [up, down, pair, up2, down2, pair2, twin]
    peers += [((rep + shift) % 16, ten) for shift in (1, 2, 14, 15)]
    for peer in peers:
        pl.semaphore_signal(barrier, inc=1, device_id=peer, device_id_type=MESH)
    pl.semaphore_wait(barrier, len(peers))

    rows, width = inputs.shape
    units = hidden.shape[1]
    blocks = 4
    tall = width // blocks
    chunk_rows = rows // 4
    shard_rows = rows // 8

    def picked(step, start, count, table):
        chosen = ids[step, pl.ds(pl.multiple_of(start, shard_rows), count), :]
        lanes = lax.broadcasted_iota(jnp.int32, (count, rows), 1)
        mask = jnp.where(chosen == lanes, 1.0, 0.0).astype(BF16)
        return jnp.dot(mask, table[...], preferred_element_type=F32)

    def fetch(step):
        def some(i, carry):
            at = pl.ds(pl.multiple_of(i * chunk_rows, chunk_rows), chunk_rows)
            inputs[at, :] = picked(step, i * chunk_rows, chunk_rows, tokens).astype(BF16)
            return carry

        lax.fori_loop(0, 4, some, 0)

    fetch(0)

    def start_cast(i, carry):
        at = pl.ds(pl.multiple_of(i * 128, 128), 128)
        for m in (0, 1):
            cast[m, at, :] = weights[m, at, :].astype(BF16)
            gone[m, at, :] = jnp.zeros((128, units), F32)
        return carry

    load[0].wait()
    load[1].wait()
    lax.fori_loop(0, width // 128, start_cast, 0)
    load[2].wait()

    def box(step, m, j, device):
        at = pl.ds(pl.multiple_of(j * tall, tall), tall)
        return pltpu.make_async_remote_copy(
            src_ref=out_box.at[step, m, at],
            dst_ref=in_box.at[step, m, at],
            send_sem=box_send.at[step, m * blocks + j],
            recv_sem=box_recv.at[step, m * blocks + j],
            device_id=device,
            device_id_type=MESH,
        )

    def inner_step(step, carry):
        ring = Exchange(
            row, side, up, down, pair, shard_rows, part, hop.at[step], mid, fin.at[step],
            give, got.at[step], error.at[step], send.at[step], recv.at[step],
        )

        def make(chunk):
            at = pl.ds(pl.multiple_of(chunk * chunk_rows, chunk_rows), chunk_rows)
            pre = jnp.dot(inputs[at, :], cast[0], preferred_element_type=F32)
            value, rise = gelu_pair(pre)
            value = value.astype(BF16)
            hidden[at, :] = value
            slope[at, :] = rise
            out = contract(value, cast[1], 1, 1)
            part[chunk] = out.astype(BF16).reshape(2, shard_rows, width)

        summed = ring.reduce(make)
        wanted = picked(step, ten * shard_rows, shard_rows, targets)
        own = pl.ds(pl.multiple_of(ten * shard_rows, shard_rows), shard_rows)
        error[step, own, :] = ((summed - wanted) * (1.0 / rows)).astype(BF16)

        def arrived(chunk):
            at = pl.ds(pl.multiple_of(chunk * chunk_rows, chunk_rows), chunk_rows)
            slide = jnp.dot(error[step, at, :], cast[1], preferred_element_type=F32)
            back[at, :] = (slide * slope[at, :]).astype(BF16)

        ring.gather(arrived)

        def update(m, left, right):
            def one(j, carry):
                at = pl.ds(pl.multiple_of(j * tall, tall), tall)
                grad = contract(left[:, at], right[...], 0, 0)
                fresh = inner_beta * moment[m, at, :] + grad
                moment[m, at, :] = fresh
                moved = gone[m, at, :] + fresh
                gone[m, at, :] = moved
                kept = weights[m, at, :] - learn_rate * fresh
                weights[m, at, :] = kept
                out_box[step, m, at, :] = jnp.where(step < 2, kept, moved).astype(BF16)

                @pl.when(step < 2)
                def _():
                    box(step, m, j, ((rep + step + 1) % 16, ten)).start()

                @pl.when((step == 2) & (core == 1 - m))
                def _():
                    box(step, m, j, twin).start()

                return carry

            lax.fori_loop(0, blocks, one, 0)

        update(1, error.at[step], hidden)
        update(0, inputs, back)
        ring.finish()

        @pl.when(step < 2)
        def _():
            fetch(step + 1)
            for m in (1, 0):

                def mix(j, carry):
                    at = pl.ds(pl.multiple_of(j * tall, tall), tall)
                    box(step, m, j, ((rep + step + 1) % 16, ten)).wait_recv()
                    mixed = 0.5 * (weights[m, at, :] + in_box[step, m, at, :].astype(F32))
                    weights[m, at, :] = mixed
                    cast[m, at, :] = mixed.astype(BF16)
                    return carry

                lax.fori_loop(0, blocks, mix, 0)

            def drain(j, carry):
                for m in (1, 0):
                    box(step, m, j, ((rep + step + 1) % 16, ten)).wait_send()
                return carry

            lax.fori_loop(0, blocks, drain, 0)

        return carry

    lax.fori_loop(0, INNER, inner_step, 0)

    store = pltpu.make_async_copy(moment, moment_out.at[0], local.at[2])
    store.start()

    ring = Exchange(
        depth, low, up2, down2, pair2, width // 8, part2, hop2, mid2, fin2,
        give2, got2, total.at[core], send2, recv2,
    )

    def join(chunk):
        at = pl.ds(pl.multiple_of(chunk * tall, tall), tall)
        box(2, core, chunk, twin).wait_recv()
        both = gone[core, at, :] + in_box[2, core, at, :].astype(F32)
        part2[chunk] = both.astype(BF16).reshape(2, tall // 2, units)

    summed = ring.reduce(join)
    own = pl.ds(pl.multiple_of((depth * 2 + low) * (width // 8), width // 8), width // 8)
    total[core, own, :] = summed.astype(BF16)

    def across(which, chunk):
        at = pl.ds(pl.multiple_of(chunk * tall, tall), tall)
        return pltpu.make_async_remote_copy(
            src_ref=total.at[which, at],
            dst_ref=total.at[which, at],
            send_sem=core_send.at[chunk],
            recv_sem=core_recv.at[chunk],
            device_id=twin,
            device_id_type=MESH,
        )

    ring.gather(lambda chunk: across(core, chunk).start())
    for chunk in range(4):
        across(1 - core, chunk).wait_recv()
    save = pltpu.make_async_copy(total, total_out, local.at[0])
    save.start()
    for chunk in range(4):
        across(core, chunk).wait_send()
        box(2, 1 - core, chunk, twin).wait_send()
    ring.finish()
    save.wait()
    store.wait()


def body(tokens, targets, row_ids, anchor, momentum, slow):
    rows, width = tokens.shape
    units = anchor.shape[2]
    shard, wide = rows // 8, width // 8
    any_spec = pl.BlockSpec(memory_space=pl.ANY)
    vmem_spec = pl.BlockSpec(memory_space=pltpu.VMEM)
    dma = pltpu.SemaphoreType.DMA
    ids = row_ids.reshape(INNER, rows, 1)
    moment, total = pl.pallas_call(
        kernel,
        name="outer_round",
        out_shape=(
            jax.ShapeDtypeStruct(momentum.shape, F32),
            jax.ShapeDtypeStruct(anchor.shape, BF16),
        ),
        in_specs=[vmem_spec, vmem_spec, vmem_spec, any_spec, any_spec],
        out_specs=(any_spec, any_spec),
        scratch_shapes=[
            pltpu.VMEM((2, width, units), F32),
            pltpu.VMEM((2, width, units), F32),
            pltpu.VMEM((2, width, units), F32),
            pltpu.VMEM((2, width, units), BF16),
            pltpu.VMEM((INNER, 2, width, units), BF16),
            pltpu.VMEM((INNER, 2, width, units), BF16),
            pltpu.VMEM((rows, width), BF16),
            pltpu.VMEM((rows, units), BF16),
            pltpu.VMEM((rows, units), F32),
            pltpu.VMEM((rows, units), BF16),
            pltpu.VMEM((4, 2, shard, width), BF16),
            pltpu.VMEM((INNER, 2, shard, width), BF16),
            pltpu.VMEM((2, shard, width), BF16),
            pltpu.VMEM((INNER, 2, 2, shard, width), BF16),
            pltpu.VMEM((shard, width), BF16),
            pltpu.VMEM((INNER, shard, width), BF16),
            pltpu.VMEM((INNER, rows, width), BF16),
            pltpu.VMEM((4, 2, wide, units), BF16),
            pltpu.VMEM((2, wide, units), BF16),
            pltpu.VMEM((2, wide, units), BF16),
            pltpu.VMEM((2, 2, wide, units), BF16),
            pltpu.VMEM((wide, units), BF16),
            pltpu.VMEM((wide, units), BF16),
            pltpu.VMEM((2, width, units), BF16),
            dma((INNER, 14)),
            dma((INNER, 14)),
            dma((14,)),
            dma((14,)),
            dma((INNER, 8)),
            dma((INNER, 8)),
            dma((4,)),
            dma((4,)),
            dma((3,)),
        ],
        compiler_params=pltpu.CompilerParams(
            collective_id=0, has_side_effects=True, vmem_limit_bytes=60 * 1024 * 1024
        ),
    )(ids, tokens, targets, anchor, momentum)
    mean = total.astype(F32) * (1.0 / lax.axis_size("replica"))
    slow_new = slow_beta * slow + mean
    anchor_new = anchor - learn_rate * slow_new
    return (anchor_new, slow_new, moment)


def solution(mesh):
    return jax.shard_map(
        body,
        mesh=mesh,
        in_specs=(
            P("replica", None),
            P("replica", None),
            P("replica", None, None),
            P(None, None, "tensor"),
            P("replica", None, None, "tensor"),
            P(None, None, "tensor"),
        ),
        out_specs=(
            P(None, None, "tensor"),
            P(None, None, "tensor"),
            P("replica", None, None, "tensor"),
        ),
        check_vma=False,
    )
```

time: 625 us -> 217 us (0.35)
  waiting for transfers between devices: 497 us -> 0 us
  Pallas kernels: 0 us -> 202 us
  matrix products: 37 us -> 0 us
  other arithmetic: 45.6 us -> 9.1 us
  local copies, waits for them, and re-layouts: 26.7 us -> 3.89 us
  between operations: 14 us -> 0.65 us
    psum x4 -> x0, waiting for transfers between devices: 431 us -> none  [the longest x3 310 us: body(): summed = lax.psum(partial_out, 'tensor')]
    pallas_call x0 -> x1, Pallas kernels: none -> 202 us  [body(): pl.pallas_call(kernel, name='outer_round', out_shape=(jax.ShapeDtypeStruc...]
    ppermute x2 -> x0, waiting for transfers between devices: 66 us -> none  [passed_along(): return lax.ppermute(block, axis, route)]
    dot_general x12 -> x0, matrix products: 37 us -> none  [the longest x3 16.7 us: body(): lax.dot_general(inputs, back, (((0,), (0,)), ((), ())), preferred_element...]
    convert_element_type x5 -> x0, other arithmetic: 22.2 us -> none  [the longest x3 12.7 us: body(): weights_bf = weights.astype(jnp.bfloat16)]
    gather x6 -> x0, local copies, waits for them, and re-layouts: 13.8 us -> none  [the longest x3 7.61 us: body(): wanted = jnp.take(targets, picks, axis=0)]
    unnamed x44 -> x3, local copies, waits for them, and re-layouts: 12.2 us -> 2.02 us
    add x1 -> x0, other arithmetic: 7.66 us -> none  [body(): moment = inner_beta * moment + jnp.stack([grad_in, grad_out])]
  transfers between devices with their start and end apart: 6 -> 0, of which waited for: 6 -> 0; matrix products, arithmetic and copies ran while one was open for 3% -> 0% of each run, Pallas kernels for 0% -> 0%
where the time goes in v2:
time: 217 us; the launch traced here: 216 us
  Pallas kernels  202 us (93%)
  other arithmetic  9.1 us (4%)
  local copies, waits for them, and re-layouts  3.89 us (2%)
    pallas_call x1, Pallas kernels, body(): pl.pallas_call(kernel, name='outer_round', out_shape=(jax.ShapeDtypeStruc...  202 us
    sub x1, other arithmetic, body(): anchor_new = anchor - learn_rate * slow_new  9.1 us

profile of v2, /device:TPU:1, one launch (start us, length us, event | category | flops | bytes accessed | tf_op | source)
XLA Modules:
  0.0 215.6 jit_solution(5192847842593374730)
XLA Ops:
  0.6 1.9 copy.9.ids
  2.5 201.9 %outer_round.1 = (f32[1,2,1024,512]{3,2,1,0:T(8,128)}, bf16[2,1024,512]{2,1,0:T(8,128)(2,1)}) custom-call(s32[3,512,1]{2,1,0:T(8,128)} %copy.9.ids, bf16[512,1024]{1,0:T(8,128)(2,1)} %tokens.1, bf16[512,1024]{1,0:T(8,128)(2,1)} %targets.1, f32[2,1024,512]{2,1,0:T(8,128)} %anchor.1, f32[1,2,1024,512]{3,2,1,0:T(8,128)} %momentum.1), custom_call_target="tpu_custom_call" | custom-call | tf_op jit(solution)/shard_map/outer_round/pallas_call | solution.py:337
  204.4 0.0 copy-start
  204.4 9.1 %multiply_subtract_fusion = (f32[2,1024,512]{2,1,0:T(8,128)}, f32[2,1024,512]{2,1,0:T(8,128)}) fusion(f32[2,1024,512]{2,1,0:T(8,128)} %anchor.1, bf16[2,1024,512]{2,1,0:T(8,128)(2,1)} %get-tuple-element.5, f32[2,1024,512]{2,1,0:T(8,128)} %param.11), kind=kLoop, calls=%fused_computation | loop fusion | flops 6291456 | bytes 18874368 | tf_op jit(solution)/shard_map/sub | solution.py:387
  213.5 0.0 copy-done
  213.6 2.0 copy.11
Async XLA Ops:
  204.4 9.1 %copy-start = (f32[1,2,1024,512]{3,2,1,0:T(8,128)S(1)}, f32[1,2,1024,512]{3,2,1,0:T(8,128)}, u32[]{:S(2)}) copy-start(f32[1,2,1024,512]{3,2,1,0:T(8,128)} %get-tuple-element.14) | copy-start | bytes 12582916

commit v3 on v2

v3 whole, which is shorter than its diff:
```python
import functools

import jax
import jax.numpy as jnp
from jax import lax
from jax.experimental import pallas as pl
from jax.experimental.pallas import tpu as pltpu
from jax.sharding import PartitionSpec as P

INNER = 3
learn_rate = 0.02
inner_beta = 0.9
slow_beta = 0.5

F32 = jnp.float32
BF16 = jnp.bfloat16
MESH = pl.DeviceIdType.MESH


def gelu_pair(pre):
    coeff = 0.7978845608028654
    square = pre * pre
    tanh_val = jnp.tanh(coeff * (pre + 0.044715 * pre * square))
    upper = 0.5 * (1.0 + tanh_val)
    value = pre * upper
    slope = upper + 0.5 * pre * (1.0 - tanh_val * tanh_val) * coeff * (
        1.0 + 3.0 * 0.044715 * square
    )
    return (value, slope)


def contract(a, b, dim_a, dim_b):
    return lax.dot_general(a, b, (((dim_a,), (dim_b,)), ((), ())), preferred_element_type=F32)


class Exchange:
    def __init__(self, pos, half, up, down, pair, block, part, hop, mid, fin, give, got, full, send, recv):
        self.pos, self.half, self.up, self.down, self.pair = pos, half, up, down, pair
        self.block, self.part, self.hop, self.mid, self.fin = block, part, hop, mid, fin
        self.give, self.got, self.full, self.send, self.recv = give, got, full, send, recv
        self.sent = []

    def copy(self, src, dst, index, device):
        return pltpu.make_async_remote_copy(
            src_ref=src,
            dst_ref=dst,
            send_sem=self.send.at[index],
            recv_sem=self.recv.at[index],
            device_id=device,
            device_id_type=MESH,
        )

    def start(self, src, dst, index, device):
        copy = self.copy(src, dst, index, device)
        copy.start()
        self.sent.append(copy)
        return copy

    def piece(self, chunk, half):
        return self.part.at[chunk, half]

    def reduce(self, make, early=None, idle=None):
        pos = self.pos
        far, above, below = (pos + 2) % 4, (pos + 1) % 4, (pos + 3) % 4
        make(far)
        first_up = self.start(self.piece(far, 0), self.hop.at[0], 0, self.up)
        first_down = self.start(self.piece(far, 1), self.hop.at[1], 1, self.down)
        if early is not None:
            early()
        make(above)
        self.start(self.piece(above, 1), self.fin.at[1, 0], 2, self.up)
        make(below)
        self.start(self.piece(below, 0), self.fin.at[0, 0], 3, self.down)
        make(pos)
        first_up.wait_recv()
        self.mid[0] = (self.part[above, 0].astype(F32) + self.hop[0].astype(F32)).astype(BF16)
        self.start(self.mid.at[0], self.fin.at[0, 1], 4, self.up)
        first_down.wait_recv()
        self.mid[1] = (self.part[below, 1].astype(F32) + self.hop[1].astype(F32)).astype(BF16)
        self.start(self.mid.at[1], self.fin.at[1, 1], 5, self.down)
        if idle is not None:
            idle()
        for copy in self.sent[2:6]:
            copy.wait_recv()
        self.give[...] = self.total(1 - self.half).astype(BF16)
        last = self.start(self.give, self.got, 6, self.pair)
        mine = self.total(self.half)
        last.wait_recv()
        return mine + self.got[...].astype(F32)

    def total(self, half):
        return (
            self.part[self.pos, half].astype(F32)
            + self.fin[half, 0].astype(F32)
            + self.fin[half, 1].astype(F32)
        )

    def slot(self, chunk, half):
        return self.full.at[pl.ds(pl.multiple_of((chunk * 2 + half) * self.block, self.block), self.block)]

    def gather(self, arrived, idle=None):
        pos, half = self.pos, self.half
        far, above, below = (pos + 2) % 4, (pos + 1) % 4, (pos + 3) % 4
        own, other = self.slot(pos, half), self.slot(pos, 1 - half)
        self.start(own, own, 7, self.pair)
        self.start(own, own, 8, self.up)
        self.start(own, own, 9, self.down)
        if idle is not None:
            idle(0)
        self.copy(other, other, 7, self.pair).wait_recv()
        self.start(other, other, 10, self.up)
        self.start(other, other, 11, self.down)
        arrived(pos, 0)
        early, late = self.slot(below, half), self.slot(above, 1 - half)
        self.copy(own, early, 8, self.up).wait_recv()
        self.start(early, early, 12, self.up)
        if idle is not None:
            idle(1)
        self.copy(own, late, 11, self.down).wait_recv()
        self.start(late, late, 13, self.down)
        self.copy(own, self.slot(above, half), 9, self.down).wait_recv()
        arrived(above, 1)
        self.copy(own, self.slot(below, 1 - half), 10, self.up).wait_recv()
        arrived(below, 2)
        self.copy(own, self.slot(far, half), 12, self.up).wait_recv()
        self.copy(own, self.slot(far, 1 - half), 13, self.down).wait_recv()
        arrived(far, 3)

    def finish(self):
        for copy in self.sent:
            copy.wait_send()


def kernel(
    ids, tokens, targets, anchor, momentum,
    moment_out, total_out,
    weights, moment, gone, cast, out_box, in_box, twin_out, twin_in,
    inputs, hidden, slope, back, want,
    near_inputs, near_hidden, near_slope, near_back, near_error, relay,
    part, hop, mid, fin, give, got, error,
    part2, hop2, mid2, fin2, give2, got2, total,
    send, recv, send2, recv2, box_send, box_recv, near_send, near_recv,
    relay_send, relay_recv, twin_send, twin_recv, core_send, core_recv, local,
):
    rep, ten = lax.axis_index("replica"), lax.axis_index("tensor")
    row, side = ten // 2, ten % 2
    low, depth, core = rep // 8, (rep // 2) % 4, rep % 2

    def plane(shift):
        return low * 8 + (depth + shift) % 4 * 2 + core

    up, down = (rep, (row + 1) % 4 * 2 + side), (rep, (row + 3) % 4 * 2 + side)
    pair = (rep, row * 2 + 1 - side)
    up2, down2 = (plane(1), ten), (plane(3), ten)
    pair2 = ((1 - low) * 8 + depth * 2 + core, ten)
    twin = (low * 8 + depth * 2 + 1 - core, ten)
    after, second = ((rep + 1) % 16, ten), ((rep + 2) % 16, ten)
    relay_end = ((plane(2) + 2) % 16, ten)
    past = (rep + 14) % 16
    relay_start = (past // 8 * 8 + ((past // 2) % 4 + 2) % 4 * 2 + core, ten)

    load = [
        pltpu.make_async_copy(anchor.at[0], weights.at[0], local.at[0]),
        pltpu.make_async_copy(anchor.at[1], weights.at[1], local.at[1]),
        pltpu.make_async_copy(momentum.at[0], moment, local.at[2]),
    ]
    for copy in load:
        copy.start()

    barrier = pltpu.get_barrier_semaphore()
    peers = [up, down, pair, up2, down2, pair2, twin, relay_end, relay_start]
    peers += [((rep + shift) % 16, ten) for shift in (1, 2, 14, 15)]
    for peer in peers:
        pl.semaphore_signal(barrier, inc=1, device_id=peer, device_id_type=MESH)
    pl.semaphore_wait(barrier, len(peers))

    rows, width = inputs.shape
    units = hidden.shape[1]
    blocks = 4
    tall = width // blocks
    chunk_rows = rows // 4
    shard_rows = rows // 8

    def remote(src, dst, send_sem, recv_sem, device):
        return pltpu.make_async_remote_copy(
            src_ref=src, dst_ref=dst, send_sem=send_sem, recv_sem=recv_sem,
            device_id=device, device_id_type=MESH,
        )

    def chunk_at(chunk):
        return pl.ds(pl.multiple_of(chunk * chunk_rows, chunk_rows), chunk_rows)

    def block_at(j):
        return pl.ds(pl.multiple_of(j * tall, tall), tall)

    def picked(step, chunk, table):
        chosen = ids[step, :, chunk_at(chunk)]
        places = lax.broadcasted_iota(jnp.int32, (rows, chunk_rows), 0)
        mask = jnp.where(chosen == places, 1.0, 0.0).astype(BF16)
        return contract(mask, table[...], 0, 0)

    def fetch(step):
        def some(i, carry):
            inputs[chunk_at(i), :] = picked(step, i, tokens).astype(BF16)
            return carry

        lax.fori_loop(0, 4, some, 0)

    def start_cast(i, carry):
        at = pl.ds(pl.multiple_of(i * 128, 128), 128)
        for m in (0, 1):
            cast[m, at, :] = weights[m, at, :].astype(BF16)
        return carry

    def decay(i, carry):
        at = pl.ds(pl.multiple_of(i * 128, 128), 128)
        for m in (0, 1):
            out_box[0, m, at, :] = (inner_beta * moment[m, at, :]).astype(BF16)
        return carry

    near_x = remote(inputs, near_inputs, near_send.at[4], near_recv.at[4], after)
    near_m = remote(out_box.at[0], in_box.at[0], near_send.at[5], near_recv.at[5], after)

    def near_piece(chunk, order):
        at = chunk_at(chunk)
        return remote(
            error.at[0, at], near_error.at[at], near_send.at[order], near_recv.at[order], after
        )

    def box(m, j):
        at = block_at(j)
        index = m * blocks + j
        return remote(
            out_box.at[1, m, at], in_box.at[1, m, at], box_send.at[index], box_recv.at[index], second
        )

    def leg(hop_index, j):
        src = out_box.at[1, 1, block_at(j)] if hop_index == 0 else relay.at[hop_index - 1, j]
        dst = in_box.at[1, 1, block_at(j)] if hop_index == 2 else relay.at[hop_index, j]
        return remote(
            src, dst, relay_send.at[hop_index, j], relay_recv.at[hop_index, j],
            relay_end if hop_index == 2 else down2,
        )

    def twin_box(j):
        at = block_at(j)
        return remote(twin_out.at[at], twin_in.at[at], twin_send.at[j], twin_recv.at[j], twin)

    fetch(0)
    near_x.start()
    load[0].wait()
    load[1].wait()
    lax.fori_loop(0, width // 128, start_cast, 0)

    def one_step(step):
        ring = Exchange(
            row, side, up, down, pair, shard_rows, part, hop.at[step], mid, fin.at[step],
            give, got.at[step], error.at[step], send.at[step], recv.at[step],
        )

        def forward(source, at, kept, rise):
            pre = jnp.dot(source[at, :], cast[0], preferred_element_type=F32)
            value, tilt = gelu_pair(pre)
            value = value.astype(BF16)
            kept[at, :] = value
            rise[at, :] = tilt
            return value

        def make(chunk):
            value = forward(inputs, chunk_at(chunk), hidden, slope)
            out = contract(value, cast[1], 1, 1)
            part[chunk] = out.astype(BF16).reshape(2, shard_rows, width)

        def early():
            load[2].wait()
            lax.fori_loop(0, width // 128, decay, 0)
            near_m.start()

        def idle():
            want[...] = picked(step, row, targets).reshape(2, shard_rows, width)

        summed = ring.reduce(make, early if step == 0 else None, idle)
        own = pl.ds(pl.multiple_of(ten * shard_rows, shard_rows), shard_rows)
        error[step, own, :] = ((summed - want[side]) * (1.0 / rows)).astype(BF16)

        def pull(source, at, rise, result):
            slide = jnp.dot(source[at, :], cast[1], preferred_element_type=F32)
            result[at, :] = (slide * rise[at, :]).astype(BF16)

        def arrived(chunk, order):
            if step == 0:
                near_piece(chunk, order).start()
            pull(error.at[step], chunk_at(chunk), slope, back)

        def near_forward(part_of):
            if part_of == 0:
                near_x.wait_recv()

            def one(i, carry):
                forward(near_inputs, chunk_at(i), near_hidden, near_slope)
                return carry

            lax.fori_loop(part_of * 2, part_of * 2 + 2, one, 0)

        ring.gather(arrived, near_forward if step == 0 else None)

        def update(m, left, right, first, last, ship):
            def one(j, carry):
                at = block_at(j)
                fresh = inner_beta * moment[m, at, :] + contract(left[:, at], right[...], 0, 0)
                moment[m, at, :] = fresh
                moved = fresh if step == 0 else gone[m, at, :] + fresh
                gone[m, at, :] = moved
                if step < 2:
                    kept = weights[m, at, :] - learn_rate * fresh
                    weights[m, at, :] = kept
                if step == 1:
                    out_box[1, m, at, :] = kept.astype(BF16)
                    ship(j).start()
                if step == 2:

                    @pl.when(core == 1 - m)
                    def _():
                        twin_out[at, :] = moved.astype(BF16)
                        twin_box(j).start()

                return carry

            lax.fori_loop(first, last, one, 0)

        def blend(m, at, other):
            mixed = 0.5 * (weights[m, at, :] + other)
            weights[m, at, :] = mixed
            cast[m, at, :] = mixed.astype(BF16)

        if step == 1:
            update(1, error.at[step], hidden, 0, 2, lambda j: leg(0, j))
            update(1, error.at[step], hidden, 2, 4, lambda j: box(1, j))
            update(0, inputs, back, 0, 4, lambda j: box(0, j))
        else:
            update(1, error.at[step], hidden, 0, 4, None)
            update(0, inputs, back, 0, 4, None)
        ring.finish()

        if step == 0:
            far, above, below = (row + 2) % 4, (row + 1) % 4, (row + 3) % 4
            for order, chunk in enumerate((row, above, below, far)):
                near_piece(chunk, order).wait_recv()
                pull(near_error, chunk_at(chunk), near_slope, near_back)
            near_m.wait_recv()
            near_x.wait_send()
            for m, left, right in ((1, near_error, near_hidden), (0, near_inputs, near_back)):

                def one(j, carry):
                    at = block_at(j)
                    grad = contract(left[:, at], right[...], 0, 0)
                    began = weights[m, at, :] + learn_rate * moment[m, at, :]
                    near = began - learn_rate * (in_box[0, m, at, :].astype(F32) + grad)
                    blend(m, at, near.astype(BF16).astype(F32))
                    return carry

                lax.fori_loop(0, blocks, one, 0)
            fetch(1)
            near_m.wait_send()
            for order, chunk in enumerate((row, above, below, far)):
                near_piece(chunk, order).wait_send()

        if step == 1:

            def take(m, j, copy):
                copy.wait_recv()
                blend(m, block_at(j), in_box[1, m, block_at(j), :].astype(F32))

            def relay_on(hop_index, j):
                leg(hop_index, j).wait_recv()
                leg(hop_index + 1, j).start()

            fetch(2)
            relay_on(0, 0)
            take(1, 2, box(1, 2))
            relay_on(0, 1)
            take(1, 3, box(1, 3))
            relay_on(1, 0)
            take(0, 0, box(0, 0))
            relay_on(1, 1)
            take(0, 1, box(0, 1))
            take(1, 0, leg(2, 0))
            take(0, 2, box(0, 2))
            take(1, 1, leg(2, 1))
            take(0, 3, box(0, 3))
            for m, j in ((1, 2), (1, 3), (0, 0), (0, 1), (0, 2), (0, 3)):
                box(m, j).wait_send()
            for hop_index in range(3):
                for j in (0, 1):
                    leg(hop_index, j).wait_send()

    for step in range(INNER):
        one_step(step)

    store = pltpu.make_async_copy(moment, moment_out.at[0], local.at[2])
    store.start()

    ring = Exchange(
        depth, low, up2, down2, pair2, width // 8, part2, hop2, mid2, fin2,
        give2, got2, total.at[core], send2, recv2,
    )

    def join(chunk):
        at = pl.ds(pl.multiple_of(chunk * tall, tall), tall)
        twin_box(chunk).wait_recv()
        both = gone[core, at, :] + twin_in[at, :].astype(F32)
        part2[chunk] = both.astype(BF16).reshape(2, tall // 2, units)

    summed = ring.reduce(join)
    own = pl.ds(pl.multiple_of((depth * 2 + low) * (width // 8), width // 8), width // 8)
    total[core, own, :] = summed.astype(BF16)

    def across(which, chunk):
        at = pl.ds(pl.multiple_of(chunk * tall, tall), tall)
        return pltpu.make_async_remote_copy(
            src_ref=total.at[which, at],
            dst_ref=total.at[which, at],
            send_sem=core_send.at[chunk],
            recv_sem=core_recv.at[chunk],
            device_id=twin,
            device_id_type=MESH,
        )

    ring.gather(lambda chunk, order: across(core, chunk).start())
    for chunk in range(4):
        across(1 - core, chunk).wait_recv()
    save = pltpu.make_async_copy(total, total_out, local.at[0])
    save.start()
    for chunk in range(4):
        across(core, chunk).wait_send()
        twin_box(chunk).wait_send()
    ring.finish()
    save.wait()
    store.wait()


def body(tokens, targets, row_ids, anchor, momentum, slow):
    rows, width = tokens.shape
    units = anchor.shape[2]
    shard, wide = rows // 8, width // 8
    any_spec = pl.BlockSpec(memory_space=pl.ANY)
    vmem_spec = pl.BlockSpec(memory_space=pltpu.VMEM)
    dma = pltpu.SemaphoreType.DMA
    ids = row_ids.reshape(INNER, 1, rows)
    moment, total = pl.pallas_call(
        kernel,
        name="outer_round",
        out_shape=(
            jax.ShapeDtypeStruct(momentum.shape, F32),
            jax.ShapeDtypeStruct(anchor.shape, BF16),
        ),
        in_specs=[vmem_spec, vmem_spec, vmem_spec, any_spec, any_spec],
        out_specs=(any_spec, any_spec),
        scratch_shapes=[
            pltpu.VMEM((2, width, units), F32),
            pltpu.VMEM((2, width, units), F32),
            pltpu.VMEM((2, width, units), F32),
            pltpu.VMEM((2, width, units), BF16),
            pltpu.VMEM((2, 2, width, units), BF16),
            pltpu.VMEM((2, 2, width, units), BF16),
            pltpu.VMEM((width, units), BF16),
            pltpu.VMEM((width, units), BF16),
            pltpu.VMEM((rows, width), BF16),
            pltpu.VMEM((rows, units), BF16),
            pltpu.VMEM((rows, units), F32),
            pltpu.VMEM((rows, units), BF16),
            pltpu.VMEM((2, shard, width), F32),
            pltpu.VMEM((rows, width), BF16),
            pltpu.VMEM((rows, units), BF16),
            pltpu.VMEM((rows, units), F32),
            pltpu.VMEM((rows, units), BF16),
            pltpu.VMEM((rows, width), BF16),
            pltpu.VMEM((2, 2, width // 4, units), BF16),
            pltpu.VMEM((4, 2, shard, width), BF16),
            pltpu.VMEM((INNER, 2, shard, width), BF16),
            pltpu.VMEM((2, shard, width), BF16),
            pltpu.VMEM((INNER, 2, 2, shard, width), BF16),
            pltpu.VMEM((shard, width), BF16),
            pltpu.VMEM((INNER, shard, width), BF16),
            pltpu.VMEM((INNER, rows, width), BF16),
            pltpu.VMEM((4, 2, wide, units), BF16),
            pltpu.VMEM((2, wide, units), BF16),
            pltpu.VMEM((2, wide, units), BF16),
            pltpu.VMEM((2, 2, wide, units), BF16),
            pltpu.VMEM((wide, units), BF16),
            pltpu.VMEM((wide, units), BF16),
            pltpu.VMEM((2, width, units), BF16),
            dma((INNER, 14)),
            dma((INNER, 14)),
            dma((14,)),
            dma((14,)),
            dma((8,)),
            dma((8,)),
            dma((6,)),
            dma((6,)),
            dma((3, 2)),
            dma((3, 2)),
            dma((4,)),
            dma((4,)),
            dma((4,)),
            dma((4,)),
            dma((3,)),
        ],
        compiler_params=pltpu.CompilerParams(
            collective_id=0, has_side_effects=True, vmem_limit_bytes=60 * 1024 * 1024
        ),
    )(ids, tokens, targets, anchor, momentum)
    mean = total.astype(F32) * (1.0 / lax.axis_size("replica"))
    slow_new = slow_beta * slow + mean
    anchor_new = anchor - learn_rate * slow_new
    return (anchor_new, slow_new, moment)


def solution(mesh):
    return jax.shard_map(
        body,
        mesh=mesh,
        in_specs=(
            P("replica", None),
            P("replica", None),
            P("replica", None, None),
            P(None, None, "tensor"),
            P("replica", None, None, "tensor"),
            P(None, None, "tensor"),
        ),
        out_specs=(
            P(None, None, "tensor"),
            P(None, None, "tensor"),
            P("replica", None, None, "tensor"),
        ),
        check_vma=False,
    )
```

time: 217 us -> 207 us (0.954)
  Pallas kernels: 202 us -> 195 us
    pallas_call x1, Pallas kernels: 202 us -> 195 us  [body(): pl.pallas_call(kernel, name='outer_round', out_shape=(jax.ShapeDtypeStruc...]
where the time goes in v3:
time: 207 us
  Pallas kernels  195 us (94%)
  other arithmetic  9.1 us (4%)
    pallas_call x1, Pallas kernels, body(): pl.pallas_call(kernel, name='outer_round', out_shape=(jax.ShapeDtypeStruc...  195 us
    sub x1, other arithmetic, body(): anchor_new = anchor - learn_rate * slow_new  9.1 us

profile of v3, /device:TPU:1, one launch (start us, length us, event | category | flops | bytes accessed | tf_op | source)
XLA Modules:
  0.0 206.6 jit_solution(1429119213783279167)
XLA Ops:
  0.6 194.8 %outer_round.1 = (f32[1,2,1024,512]{3,2,1,0:T(8,128)}, bf16[2,1024,512]{2,1,0:T(8,128)(2,1)}) custom-call(s32[3,1,512]{2,1,0:T(1,128)} %bitcast.1, bf16[512,1024]{1,0:T(8,128)(2,1)} %tokens.1, bf16[512,1024]{1,0:T(8,128)(2,1)} %targets.1, f32[2,1024,512]{2,1,0:T(8,128)} %anchor.1, f32[1,2,1024,512]{3,2,1,0:T(8,128)} %momentum.1), custom_call_target="tpu_custom_call" | custom-call | tf_op jit(solution)/shard_map/outer_round/pallas_call | solution.py:450
  195.5 0.0 copy-start
  195.5 9.1 %multiply_subtract_fusion = (f32[2,1024,512]{2,1,0:T(8,128)}, f32[2,1024,512]{2,1,0:T(8,128)}) fusion(f32[2,1024,512]{2,1,0:T(8,128)} %anchor.1, bf16[2,1024,512]{2,1,0:T(8,128)(2,1)} %get-tuple-element.5, f32[2,1024,512]{2,1,0:T(8,128)} %param.11), kind=kLoop, calls=%fused_computation | loop fusion | flops 6291456 | bytes 18874368 | tf_op jit(solution)/shard_map/sub | solution.py:515
  204.6 0.0 copy-done
  204.6 2.0 copy.10
Async XLA Ops:
  195.5 9.1 %copy-start = (f32[1,2,1024,512]{3,2,1,0:T(8,128)S(1)}, f32[1,2,1024,512]{3,2,1,0:T(8,128)}, u32[]{:S(2)}) copy-start(f32[1,2,1024,512]{3,2,1,0:T(8,128)} %get-tuple-element.14) | copy-start | bytes 12582916

commit v4 on v3

--- a/solution.py
+++ b/solution.py
@@ -34,97 +34,112 @@
 
 
 class Exchange:
-    def __init__(self, pos, half, up, down, pair, block, part, hop, mid, fin, give, got, full, send, recv):
-        self.pos, self.half, self.up, self.down, self.pair = pos, half, up, down, pair
-        self.block, self.part, self.hop, self.mid, self.fin = block, part, hop, mid, fin
+    def __init__(self, pos, half, at, block, part, hop, mid, fin, give, got, full, send, recv):
+        self.pos, self.half, self.block = pos, half, block
+        self.part, self.hop, self.mid, self.fin = part, hop, mid, fin
         self.give, self.got, self.full, self.send, self.recv = give, got, full, send, recv
+        self.far, self.above, self.below = (pos + 2) % 4, (pos + 1) % 4, (pos + 3) % 4
+        self.first_of = at(self.above, 0)
+        self.second_of = at(self.below, 1)
+        self.up, self.down = at(self.above, half), at(self.below, half)
+        self.up_across, self.down_across = at(self.above, 1 - half), at(self.below, 1 - half)
+        self.pair = at(pos, 1 - half)
         self.sent = []
 
-    def copy(self, src, dst, index, device):
+    def peers(self):
+        return [self.up, self.down, self.up_across, self.down_across, self.pair]
+
+    def copy(self, src, dst, index, device, landing=None):
         return pltpu.make_async_remote_copy(
             src_ref=src,
             dst_ref=dst,
             send_sem=self.send.at[index],
-            recv_sem=self.recv.at[index],
+            recv_sem=self.recv.at[index if landing is None else landing],
             device_id=device,
             device_id_type=MESH,
         )
 
-    def start(self, src, dst, index, device):
-        copy = self.copy(src, dst, index, device)
+    def start(self, src, dst, index, device, landing=None):
+        copy = self.copy(src, dst, index, device, landing)
         copy.start()
         self.sent.append(copy)
         return copy
 
-    def piece(self, chunk, half):
-        return self.part.at[chunk, half]
-
-    def reduce(self, make, early=None, idle=None):
-        pos = self.pos
-        far, above, below = (pos + 2) % 4, (pos + 1) % 4, (pos + 3) % 4
-        make(far)
-        first_up = self.start(self.piece(far, 0), self.hop.at[0], 0, self.up)
-        first_down = self.start(self.piece(far, 1), self.hop.at[1], 1, self.down)
-        if early is not None:
-            early()
-        make(above)
-        self.start(self.piece(above, 1), self.fin.at[1, 0], 2, self.up)
-        make(below)
-        self.start(self.piece(below, 0), self.fin.at[0, 0], 3, self.down)
+    def reduce(self, make, idle=None, between=lambda: None):
+        pos, half, part, fin, mid = self.pos, self.half, self.part, self.fin, self.mid
+        make(self.far)
+        first_up = self.start(part.at[self.far, 0], self.hop.at[0], 0, self.up)
+        first_down = self.start(part.at[self.far, 1], self.hop.at[1], 1, self.down)
+        between()
+        make(self.above)
+        direct_up = self.start(part.at[self.above, 1], fin.at[1, 0], 2, self.up)
+        between()
+        make(self.below)
+        direct_down = self.start(part.at[self.below, 0], fin.at[0, 0], 3, self.down)
+        between()
         make(pos)
+        between()
         first_up.wait_recv()
-        self.mid[0] = (self.part[above, 0].astype(F32) + self.hop[0].astype(F32)).astype(BF16)
-        self.start(self.mid.at[0], self.fin.at[0, 1], 4, self.up)
+        mid[0] = (part[self.above, 0].astype(F32) + self.hop[0].astype(F32)).astype(BF16)
+        self.start(mid.at[0], fin.at[half, 1], 4, self.first_of, 4 + half)
+        between()
         first_down.wait_recv()
-        self.mid[1] = (self.part[below, 1].astype(F32) + self.hop[1].astype(F32)).astype(BF16)
-        self.start(self.mid.at[1], self.fin.at[1, 1], 5, self.down)
+        mid[1] = (part[self.below, 1].astype(F32) + self.hop[1].astype(F32)).astype(BF16)
+        self.start(mid.at[1], fin.at[half, 1], 5, self.second_of, 4 + half)
+        between()
         if idle is not None:
             idle()
-        for copy in self.sent[2:6]:
-            copy.wait_recv()
-        self.give[...] = self.total(1 - self.half).astype(BF16)
+        direct_up.wait_recv()
+        direct_down.wait_recv()
+        self.give[...] = self.near_total(1 - half).astype(BF16)
         last = self.start(self.give, self.got, 6, self.pair)
-        mine = self.total(self.half)
+        mine = self.near_total(half)
+        between()
+        for plane in (0, 1):
+            self.copy(mid.at[0], fin.at[plane, 1], 4, self.first_of, 4 + plane).wait_recv()
+        mine = mine + fin[0, 1].astype(F32) + fin[1, 1].astype(F32)
         last.wait_recv()
         return mine + self.got[...].astype(F32)
 
-    def total(self, half):
-        return (
-            self.part[self.pos, half].astype(F32)
-            + self.fin[half, 0].astype(F32)
-            + self.fin[half, 1].astype(F32)
-        )
+    def near_total(self, half):
+        return self.part[self.pos, half].astype(F32) + self.fin[half, 0].astype(F32)
 
     def slot(self, chunk, half):
         return self.full.at[pl.ds(pl.multiple_of((chunk * 2 + half) * self.block, self.block), self.block)]
 
-    def gather(self, arrived, idle=None):
-        pos, half = self.pos, self.half
-        far, above, below = (pos + 2) % 4, (pos + 1) % 4, (pos + 3) % 4
-        own, other = self.slot(pos, half), self.slot(pos, 1 - half)
-        self.start(own, own, 7, self.pair)
+    def open(self):
+        own = self.slot(self.pos, self.half)
         self.start(own, own, 8, self.up)
         self.start(own, own, 9, self.down)
-        if idle is not None:
-            idle(0)
-        self.copy(other, other, 7, self.pair).wait_recv()
-        self.start(other, other, 10, self.up)
-        self.start(other, other, 11, self.down)
-        arrived(pos, 0)
-        early, late = self.slot(below, half), self.slot(above, 1 - half)
-        self.copy(own, early, 8, self.up).wait_recv()
+        self.start(own, own, 11, self.down_across)
+        self.start(own, own, 10, self.up_across)
+        self.start(own, own, 7, self.pair)
+
+    def await_slot(self, chunk, half, index):
+        slot = self.slot(chunk, half)
+        self.copy(slot, slot, index, self.pair).wait_recv()
+        return slot
+
+    def pass_on(self):
+        early = self.await_slot(self.below, self.half, 8)
         self.start(early, early, 12, self.up)
-        if idle is not None:
-            idle(1)
-        self.copy(own, late, 11, self.down).wait_recv()
+        late = self.await_slot(self.above, 1 - self.half, 11)
         self.start(late, late, 13, self.down)
-        self.copy(own, self.slot(above, half), 9, self.down).wait_recv()
-        arrived(above, 1)
-        self.copy(own, self.slot(below, 1 - half), 10, self.up).wait_recv()
-        arrived(below, 2)
-        self.copy(own, self.slot(far, half), 12, self.up).wait_recv()
-        self.copy(own, self.slot(far, 1 - half), 13, self.down).wait_recv()
-        arrived(far, 3)
+
+    def collect(self, arrived, between=lambda: None):
+        half = self.half
+        self.await_slot(self.pos, 1 - half, 7)
+        arrived(self.pos)
+        between()
+        self.await_slot(self.above, half, 9)
+        arrived(self.above)
+        between()
+        self.await_slot(self.below, 1 - half, 10)
+        arrived(self.below)
+        between()
+        self.await_slot(self.far, half, 12)
+        self.await_slot(self.far, 1 - half, 13)
+        arrived(self.far)
 
     def finish(self):
         for copy in self.sent:
@@ -139,7 +154,7 @@
     near_inputs, near_hidden, near_slope, near_back, near_error, relay,
     part, hop, mid, fin, give, got, error,
     part2, hop2, mid2, fin2, give2, got2, total,
-    send, recv, send2, recv2, box_send, box_recv, near_send, near_recv,
+    send, recv, send2, recv2, send3, recv3, box_send, box_recv, near_send, near_recv,
     relay_send, relay_recv, twin_send, twin_recv, core_send, core_recv, local,
 ):
     rep, ten = lax.axis_index("replica"), lax.axis_index("tensor")
@@ -149,10 +164,13 @@
     def plane(shift):
         return low * 8 + (depth + shift) % 4 * 2 + core
 
-    up, down = (rep, (row + 1) % 4 * 2 + side), (rep, (row + 3) % 4 * 2 + side)
-    pair = (rep, row * 2 + 1 - side)
+    def tensor_at(pos, half):
+        return (rep, pos * 2 + half)
+
+    def mean_at(pos, half):
+        return (half * 8 + pos * 2 + core, ten)
+
     up2, down2 = (plane(1), ten), (plane(3), ten)
-    pair2 = ((1 - low) * 8 + depth * 2 + core, ten)
     twin = (low * 8 + depth * 2 + 1 - core, ten)
     after, second = ((rep + 1) % 16, ten), ((rep + 2) % 16, ten)
     relay_end = ((plane(2) + 2) % 16, ten)
@@ -167,19 +185,33 @@
     for copy in load:
         copy.start()
 
+    shard_rows = inputs.shape[0] // 8
+    mean_ring = Exchange(
+        depth, low, mean_at, inputs.shape[1] // 8, part2, hop2, mid2, fin2,
+        give2, got2, total.at[core], send2, recv2,
+    )
+    rings = [
+        Exchange(
+            row, side, tensor_at, shard_rows, part, hop.at[step], mid, fin.at[step],
+            give, got.at[step], error.at[step], send.at[step], recv.at[step],
+        )
+        for step in range(INNER)
+    ]
+    near_ring = Exchange(
+        row, side, tensor_at, shard_rows, part, None, mid, None,
+        give, None, near_error, send3, recv3,
+    )
     barrier = pltpu.get_barrier_semaphore()
-    peers = [up, down, pair, up2, down2, pair2, twin, relay_end, relay_start]
+    peers = rings[0].peers() + mean_ring.peers() + [twin, relay_end, relay_start]
     peers += [((rep + shift) % 16, ten) for shift in (1, 2, 14, 15)]
     for peer in peers:
         pl.semaphore_signal(barrier, inc=1, device_id=peer, device_id_type=MESH)
-    pl.semaphore_wait(barrier, len(peers))
 
     rows, width = inputs.shape
     units = hidden.shape[1]
     blocks = 4
     tall = width // blocks
     chunk_rows = rows // 4
-    shard_rows = rows // 8
 
     def remote(src, dst, send_sem, recv_sem, device):
         return pltpu.make_async_remote_copy(
@@ -212,20 +244,40 @@
             cast[m, at, :] = weights[m, at, :].astype(BF16)
         return carry
 
-    def decay(i, carry):
-        at = pl.ds(pl.multiple_of(i * 128, 128), 128)
-        for m in (0, 1):
+    def near_x(i):
+        at = chunk_at(i)
+        return remote(inputs.at[at], near_inputs.at[at], near_send.at[8 + i], near_recv.at[8 + i], after)
+
+    def near_m(m, j):
+        at = block_at(j)
+        index = m * blocks + j
+        return remote(
+            out_box.at[0, m, at], in_box.at[0, m, at], near_send.at[index], near_recv.at[index], after
+        )
+
+    def near_shard():
+        own = pl.ds(pl.multiple_of(ten * shard_rows, shard_rows), shard_rows)
+        return remote(error.at[0, own], near_error.at[own], near_send.at[12], near_recv.at[12], after)
+
+    pieces = [("x", 0, i) for i in range(4)] + [("m", m, j) for m in (1, 0) for j in range(4)]
+
+    def drip():
+        if not pieces:
+            return
+        kind, m, j = pieces.pop(0)
+        if kind == "x":
+            near_x(j).start()
+            return
+        if (m, j) == (1, 0):
+            load[2].wait()
+
+        def decay(i, carry):
+            at = pl.ds(pl.multiple_of(j * tall + i * 64, 64), 64)
             out_box[0, m, at, :] = (inner_beta * moment[m, at, :]).astype(BF16)
-        return carry
-
-    near_x = remote(inputs, near_inputs, near_send.at[4], near_recv.at[4], after)
-    near_m = remote(out_box.at[0], in_box.at[0], near_send.at[5], near_recv.at[5], after)
-
-    def near_piece(chunk, order):
-        at = chunk_at(chunk)
-        return remote(
-            error.at[0, at], near_error.at[at], near_send.at[order], near_recv.at[order], after
-        )
+            return carry
+
+        lax.fori_loop(0, tall // 64, decay, 0)
+        near_m(m, j).start()
 
     def box(m, j):
         at = block_at(j)
@@ -247,16 +299,14 @@
         return remote(twin_out.at[at], twin_in.at[at], twin_send.at[j], twin_recv.at[j], twin)
 
     fetch(0)
-    near_x.start()
     load[0].wait()
     load[1].wait()
     lax.fori_loop(0, width // 128, start_cast, 0)
+    pl.semaphore_wait(barrier, len(peers))
+    drip()
 
     def one_step(step):
-        ring = Exchange(
-            row, side, up, down, pair, shard_rows, part, hop.at[step], mid, fin.at[step],
-            give, got.at[step], error.at[step], send.at[step], recv.at[step],
-        )
+        ring = rings[step]
 
         def forward(source, at, kept, rise):
             pre = jnp.dot(source[at, :], cast[0], preferred_element_type=F32)
@@ -271,15 +321,10 @@
             out = contract(value, cast[1], 1, 1)
             part[chunk] = out.astype(BF16).reshape(2, shard_rows, width)
 
-        def early():
-            load[2].wait()
-            lax.fori_loop(0, width // 128, decay, 0)
-            near_m.start()
-
         def idle():
             want[...] = picked(step, row, targets).reshape(2, shard_rows, width)
 
-        summed = ring.reduce(make, early if step == 0 else None, idle)
+        summed = ring.reduce(make, idle, drip if step == 0 else lambda: None)
         own = pl.ds(pl.multiple_of(ten * shard_rows, shard_rows), shard_rows)
         error[step, own, :] = ((summed - want[side]) * (1.0 / rows)).astype(BF16)
 
@@ -287,14 +332,12 @@
             slide = jnp.dot(source[at, :], cast[1], preferred_element_type=F32)
             result[at, :] = (slide * rise[at, :]).astype(BF16)
 
-        def arrived(chunk, order):
-            if step == 0:
-                near_piece(chunk, order).start()
+        def arrived(chunk):
             pull(error.at[step], chunk_at(chunk), slope, back)
 
         def near_forward(part_of):
-            if part_of == 0:
-                near_x.wait_recv()
+            for i in (part_of * 2, part_of * 2 + 1):
+                near_x(i).wait_recv()
 
             def one(i, carry):
                 forward(near_inputs, chunk_at(i), near_hidden, near_slope)
@@ -302,7 +345,24 @@
 
             lax.fori_loop(part_of * 2, part_of * 2 + 2, one, 0)
 
-        ring.gather(arrived, near_forward if step == 0 else None)
+        ring.open()
+        if step == 0:
+            near_shard().start()
+            drip()
+            near_forward(0)
+            drip()
+            ring.pass_on()
+            near_shard().wait_recv()
+            near_ring.open()
+            drip()
+            ring.collect(arrived, drip)
+            while pieces:
+                drip()
+            near_ring.pass_on()
+            near_forward(1)
+        else:
+            ring.pass_on()
+            ring.collect(arrived)
 
         def update(m, left, right, first, last, ship):
             def one(j, carry):
@@ -343,12 +403,15 @@
         ring.finish()
 
         if step == 0:
-            far, above, below = (row + 2) % 4, (row + 1) % 4, (row + 3) % 4
-            for order, chunk in enumerate((row, above, below, far)):
-                near_piece(chunk, order).wait_recv()
-                pull(near_error, chunk_at(chunk), near_slope, near_back)
-            near_m.wait_recv()
-            near_x.wait_send()
+            for i in range(4):
+                near_x(i).wait_send()
+            fetch(1)
+            near_ring.collect(
+                lambda chunk: pull(near_error, chunk_at(chunk), near_slope, near_back)
+            )
+            for m in (1, 0):
+                for j in range(blocks):
+                    near_m(m, j).wait_recv()
             for m, left, right in ((1, near_error, near_hidden), (0, near_inputs, near_back)):
 
                 def one(j, carry):
@@ -360,10 +423,11 @@
                     return carry
 
                 lax.fori_loop(0, blocks, one, 0)
-            fetch(1)
-            near_m.wait_send()
-            for order, chunk in enumerate((row, above, below, far)):
-                near_piece(chunk, order).wait_send()
+            for m in (1, 0):
+                for j in range(blocks):
+                    near_m(m, j).wait_send()
+            near_shard().wait_send()
+            near_ring.finish()
 
         if step == 1:
 
@@ -400,10 +464,7 @@
     store = pltpu.make_async_copy(moment, moment_out.at[0], local.at[2])
     store.start()
 
-    ring = Exchange(
-        depth, low, up2, down2, pair2, width // 8, part2, hop2, mid2, fin2,
-        give2, got2, total.at[core], send2, recv2,
-    )
+    ring = mean_ring
 
     def join(chunk):
         at = pl.ds(pl.multiple_of(chunk * tall, tall), tall)
@@ -426,7 +487,9 @@
             device_id_type=MESH,
         )
 
-    ring.gather(lambda chunk, order: across(core, chunk).start())
+    ring.open()
+    ring.pass_on()
+    ring.collect(lambda chunk: across(core, chunk).start())
     for chunk in range(4):
         across(1 - core, chunk).wait_recv()
     save = pltpu.make_async_copy(total, total_out, local.at[0])
@@ -494,10 +557,12 @@
             dma((INNER, 14)),
             dma((14,)),
             dma((14,)),
+            dma((14,)),
+            dma((14,)),
             dma((8,)),
             dma((8,)),
-            dma((6,)),
-            dma((6,)),
+            dma((13,)),
+            dma((13,)),
             dma((3, 2)),
             dma((3, 2)),
             dma((4,)),

time: 207 us -> 201 us (0.971)
  Pallas kernels: 195 us -> 189 us
    pallas_call x1, Pallas kernels: 195 us -> 189 us  [body(): pl.pallas_call(kernel, name='outer_round', out_shape=(jax.ShapeDtypeStruc...]
where the time goes in v4:
time: 201 us
  Pallas kernels  189 us (94%)
  other arithmetic  9.1 us (5%)
  local copies, waits for them, and re-layouts  2.02 us (1%)
    pallas_call x1, Pallas kernels, body(): pl.pallas_call(kernel, name='outer_round', out_shape=(jax.ShapeDtypeStruc...  189 us
    sub x1, other arithmetic, body(): anchor_new = anchor - learn_rate * slow_new  9.1 us

profile of v4, /device:TPU:1, one launch (start us, length us, event | category | flops | bytes accessed | tf_op | source)
XLA Modules:
  0.0 200.6 jit_solution(9911951897371390388)
XLA Ops:
  0.6 188.8 %outer_round.1 = (f32[1,2,1024,512]{3,2,1,0:T(8,128)}, bf16[2,1024,512]{2,1,0:T(8,128)(2,1)}) custom-call(s32[3,1,512]{2,1,0:T(1,128)} %bitcast.1, bf16[512,1024]{1,0:T(8,128)(2,1)} %tokens.1, bf16[512,1024]{1,0:T(8,128)(2,1)} %targets.1, f32[2,1024,512]{2,1,0:T(8,128)} %anchor.1, f32[1,2,1024,512]{3,2,1,0:T(8,128)} %momentum.1), custom_call_target="tpu_custom_call" | custom-call | tf_op jit(solution)/shard_map/outer_round/pallas_call | solution.py:513
  189.5 0.0 copy-start
  189.5 9.1 %multiply_subtract_fusion = (f32[2,1024,512]{2,1,0:T(8,128)}, f32[2,1024,512]{2,1,0:T(8,128)}) fusion(f32[2,1024,512]{2,1,0:T(8,128)} %anchor.1, bf16[2,1024,512]{2,1,0:T(8,128)(2,1)} %get-tuple-element.5, f32[2,1024,512]{2,1,0:T(8,128)} %param.11), kind=kLoop, calls=%fused_computation | loop fusion | flops 6291456 | bytes 18874368 | tf_op jit(solution)/shard_map/sub | solution.py:580
  198.6 0.0 copy-done
  198.6 2.0 %copy.10 = f32[1,2,1024,512]{3,2,1,0:T(8,128)} copy(f32[1,2,1024,512]{3,2,1,0:T(8,128)S(1)} %copy-done) | data formatting | bytes 8388608
Async XLA Ops:
  189.5 9.1 %copy-start = (f32[1,2,1024,512]{3,2,1,0:T(8,128)S(1)}, f32[1,2,1024,512]{3,2,1,0:T(8,128)}, u32[]{:S(2)}) copy-start(f32[1,2,1024,512]{3,2,1,0:T(8,128)} %get-tuple-element.14) | copy-start | bytes 12582916

commit v5 on v4

--- a/solution.py
+++ b/solution.py
@@ -86,7 +86,6 @@
         first_down.wait_recv()
         mid[1] = (part[self.below, 1].astype(F32) + self.hop[1].astype(F32)).astype(BF16)
         self.start(mid.at[1], fin.at[half, 1], 5, self.second_of, 4 + half)
-        between()
         if idle is not None:
             idle()
         direct_up.wait_recv()
@@ -94,7 +93,6 @@
         self.give[...] = self.near_total(1 - half).astype(BF16)
         last = self.start(self.give, self.got, 6, self.pair)
         mine = self.near_total(half)
-        between()
         for plane in (0, 1):
             self.copy(mid.at[0], fin.at[plane, 1], 4, self.first_of, 4 + plane).wait_recv()
         mine = mine + fin[0, 1].astype(F32) + fin[1, 1].astype(F32)
@@ -145,16 +143,21 @@
         for copy in self.sent:
             copy.wait_send()
 
+    def finish_gather(self):
+        for index in range(7, 14):
+            slot = self.slot(self.pos, self.half)
+            self.copy(slot, slot, index, self.pair).wait_send()
+
 
 def kernel(
     ids, tokens, targets, anchor, momentum,
     moment_out, total_out,
     weights, moment, gone, cast, out_box, in_box, twin_out, twin_in,
     inputs, hidden, slope, back, want,
-    near_inputs, near_hidden, near_slope, near_back, near_error, relay,
+    near_inputs, near_hidden, near_slope, near_back, near_error, relay, carried,
     part, hop, mid, fin, give, got, error,
     part2, hop2, mid2, fin2, give2, got2, total,
-    send, recv, send2, recv2, send3, recv3, box_send, box_recv, near_send, near_recv,
+    send, recv, send2, recv2, send3, recv3, box_send, box_recv, near_send, near_recv, turn_send, turn_recv,
     relay_send, relay_recv, twin_send, twin_recv, core_send, core_recv, local,
 ):
     rep, ten = lax.axis_index("replica"), lax.axis_index("tensor")
@@ -175,6 +178,11 @@
     after, second = ((rep + 1) % 16, ten), ((rep + 2) % 16, ten)
     relay_end = ((plane(2) + 2) % 16, ten)
     past = (rep + 14) % 16
+    ships = (depth != 3) | (core != 1)
+    hears = (depth != 0) | (core != 0)
+    turner = (low * 8 + (depth + 1) % 4 * 2 + 1 - core, ten)
+    turned = (low * 8 + (depth + 3) % 4 * 2 + 1 - core, ten)
+    beside = ((1 - low) * 8 + depth * 2 + core, ten)
     relay_start = (past // 8 * 8 + ((past // 2) % 4 + 2) % 4 * 2 + core, ten)
 
     load = [
@@ -202,7 +210,7 @@
         give, None, near_error, send3, recv3,
     )
     barrier = pltpu.get_barrier_semaphore()
-    peers = rings[0].peers() + mean_ring.peers() + [twin, relay_end, relay_start]
+    peers = rings[0].peers() + mean_ring.peers() + [twin, relay_end, relay_start, turner, turned]
     peers += [((rep + shift) % 16, ten) for shift in (1, 2, 14, 15)]
     for peer in peers:
         pl.semaphore_signal(barrier, inc=1, device_id=peer, device_id_type=MESH)
@@ -265,19 +273,43 @@
         if not pieces:
             return
         kind, m, j = pieces.pop(0)
-        if kind == "x":
-            near_x(j).start()
-            return
-        if (m, j) == (1, 0):
+        if (kind, m, j) == ("m", 1, 0):
             load[2].wait()
 
-        def decay(i, carry):
-            at = pl.ds(pl.multiple_of(j * tall + i * 64, 64), 64)
-            out_box[0, m, at, :] = (inner_beta * moment[m, at, :]).astype(BF16)
-            return carry
-
-        lax.fori_loop(0, tall // 64, decay, 0)
-        near_m(m, j).start()
+        @pl.when(ships)
+        def _():
+            if kind == "x":
+                near_x(j).start()
+                return
+
+            def decay(i, carry):
+                at = pl.ds(pl.multiple_of(j * tall + i * 64, 64), 64)
+                out_box[0, m, at, :] = (inner_beta * moment[m, at, :]).astype(BF16)
+                return carry
+
+            lax.fori_loop(0, tall // 64, decay, 0)
+            near_m(m, j).start()
+
+    def straight(m, j):
+        at = block_at(j)
+        index = m * blocks + j
+        return remote(
+            out_box.at[0, m, at], in_box.at[0, m, at], turn_send.at[index], turn_recv.at[index], after
+        )
+
+    def turn_first(m, j):
+        index, place = m * blocks + j, m * 2 + j // 2
+        return remote(
+            out_box.at[0, m, block_at(j)], carried.at[place],
+            turn_send.at[index], turn_recv.at[8 + place], turner,
+        )
+
+    def turn_second(m, j):
+        index, place = m * blocks + j, m * 2 + j // 2
+        return remote(
+            carried.at[place], in_box.at[0, m, block_at(j)],
+            turn_send.at[8 + place], turn_recv.at[index], beside,
+        )
 
     def box(m, j):
         at = block_at(j)
@@ -347,19 +379,35 @@
 
         ring.open()
         if step == 0:
-            near_shard().start()
+
+            @pl.when(ships)
+            def _():
+                near_shard().start()
+
             drip()
-            near_forward(0)
+
+            @pl.when(hears)
+            def _():
+                near_forward(0)
+
             drip()
             ring.pass_on()
-            near_shard().wait_recv()
-            near_ring.open()
+
+            @pl.when(hears)
+            def _():
+                near_shard().wait_recv()
+                near_ring.open()
+
             drip()
             ring.collect(arrived, drip)
             while pieces:
                 drip()
-            near_ring.pass_on()
-            near_forward(1)
+
+            @pl.when(hears)
+            def _():
+                near_ring.pass_on()
+                near_forward(1)
+
         else:
             ring.pass_on()
             ring.collect(arrived)
@@ -374,6 +422,20 @@
                 if step < 2:
                     kept = weights[m, at, :] - learn_rate * fresh
                     weights[m, at, :] = kept
+                if step == 0:
+
+                    @pl.when(jnp.logical_not(ships))
+                    def _():
+                        out_box[0, m, at, :] = kept.astype(BF16)
+
+                        @pl.when(j % 2 == 0)
+                        def _():
+                            straight(m, j).start()
+
+                        @pl.when(j % 2 == 1)
+                        def _():
+                            turn_first(m, j).start()
+
                 if step == 1:
                     out_box[1, m, at, :] = kept.astype(BF16)
                     ship(j).start()
@@ -397,37 +459,90 @@
             update(1, error.at[step], hidden, 0, 2, lambda j: leg(0, j))
             update(1, error.at[step], hidden, 2, 4, lambda j: box(1, j))
             update(0, inputs, back, 0, 4, lambda j: box(0, j))
-        else:
+        elif step == 0:
             update(1, error.at[step], hidden, 0, 4, None)
             update(0, inputs, back, 0, 4, None)
+        else:
+            @pl.when(core == 0)
+            def _():
+                update(1, error.at[step], hidden, 0, 4, None)
+                update(0, inputs, back, 0, 4, None)
+
+            @pl.when(core == 1)
+            def _():
+                update(0, inputs, back, 0, 4, None)
+                update(1, error.at[step], hidden, 0, 4, None)
+
         ring.finish()
 
         if step == 0:
-            for i in range(4):
-                near_x(i).wait_send()
+
+            @pl.when(ships)
+            def _():
+                for i in range(4):
+                    near_x(i).wait_send()
+
             fetch(1)
-            near_ring.collect(
-                lambda chunk: pull(near_error, chunk_at(chunk), near_slope, near_back)
-            )
-            for m in (1, 0):
-                for j in range(blocks):
-                    near_m(m, j).wait_recv()
-            for m, left, right in ((1, near_error, near_hidden), (0, near_inputs, near_back)):
-
-                def one(j, carry):
-                    at = block_at(j)
-                    grad = contract(left[:, at], right[...], 0, 0)
-                    began = weights[m, at, :] + learn_rate * moment[m, at, :]
-                    near = began - learn_rate * (in_box[0, m, at, :].astype(F32) + grad)
-                    blend(m, at, near.astype(BF16).astype(F32))
-                    return carry
-
-                lax.fori_loop(0, blocks, one, 0)
-            for m in (1, 0):
-                for j in range(blocks):
-                    near_m(m, j).wait_send()
-            near_shard().wait_send()
-            near_ring.finish()
+
+            @pl.when(hears)
+            def _():
+                near_ring.collect(
+                    lambda chunk: pull(near_error, chunk_at(chunk), near_slope, near_back)
+                )
+                for m in (1, 0):
+                    for j in range(blocks):
+                        near_m(m, j).wait_recv()
+                for m, left, right in ((1, near_error, near_hidden), (0, near_inputs, near_back)):
+
+                    def one(j, carry):
+                        at = block_at(j)
+                        grad = contract(left[:, at], right[...], 0, 0)
+                        began = weights[m, at, :] + learn_rate * moment[m, at, :]
+                        near = began - learn_rate * (in_box[0, m, at, :].astype(F32) + grad)
+                        blend(m, at, near.astype(BF16).astype(F32))
+                        return carry
+
+                    lax.fori_loop(0, blocks, one, 0)
+                near_ring.finish_gather()
+
+            @pl.when(jnp.logical_not(hears))
+            def _():
+                def pass_turn(m, j):
+                    turn_first(m, j).wait_recv()
+                    turn_second(m, j).start()
+
+                def take_turn(m, j):
+                    straight(m, j).wait_recv()
+                    blend(m, block_at(j), in_box[0, m, block_at(j), :].astype(F32))
+
+                pass_turn(1, 1)
+                take_turn(1, 0)
+                pass_turn(1, 3)
+                take_turn(1, 2)
+                take_turn(1, 1)
+                pass_turn(0, 1)
+                take_turn(0, 0)
+                take_turn(1, 3)
+                pass_turn(0, 3)
+                take_turn(0, 2)
+                take_turn(0, 1)
+                take_turn(0, 3)
+                for m in (1, 0):
+                    for j in (1, 3):
+                        turn_second(m, j).wait_send()
+
+            @pl.when(ships)
+            def _():
+                for m in (1, 0):
+                    for j in range(blocks):
+                        near_m(m, j).wait_send()
+                near_shard().wait_send()
+
+            @pl.when(jnp.logical_not(ships))
+            def _():
+                for m in (1, 0):
+                    for j in range(blocks):
+                        straight(m, j).wait_send()
 
         if step == 1:
 
@@ -539,6 +654,7 @@
             pltpu.VMEM((rows, units), BF16),
             pltpu.VMEM((rows, width), BF16),
             pltpu.VMEM((2, 2, width // 4, units), BF16),
+            pltpu.VMEM((4, width // 4, units), BF16),
             pltpu.VMEM((4, 2, shard, width), BF16),
             pltpu.VMEM((INNER, 2, shard, width), BF16),
             pltpu.VMEM((2, shard, width), BF16),
@@ -563,6 +679,8 @@
             dma((8,)),
             dma((13,)),
             dma((13,)),
+            dma((12,)),
+            dma((12,)),
             dma((3, 2)),
             dma((3, 2)),
             dma((4,)),
@@ -572,7 +690,7 @@
             dma((3,)),
         ],
         compiler_params=pltpu.CompilerParams(
-            collective_id=0, has_side_effects=True, vmem_limit_bytes=60 * 1024 * 1024
+            collective_id=0, has_side_effects=True, vmem_limit_bytes=46 * 1024 * 1024
         ),
     )(ids, tokens, targets, anchor, momentum)
     mean = total.astype(F32) * (1.0 / lax.axis_size("replica"))

time: 201 us -> 186 us (0.925)
  Pallas kernels: 189 us -> 174 us
  other arithmetic: 9.1 us -> 4.66 us
  local copies, waits for them, and re-layouts: 2.02 us -> 5.16 us
    pallas_call x1, Pallas kernels: 189 us -> 174 us  [body(): pl.pallas_call(kernel, name='outer_round', out_shape=(jax.ShapeDtypeStruc...]
    sub x1, other arithmetic: 9.1 us -> 4.66 us  [body(): anchor_new = anchor - learn_rate * slow_new]
    unnamed x3 -> x13, local copies, waits for them, and re-layouts: 2.02 us -> 5.16 us
where the time goes in v5:
time: 186 us; the launch traced here: 184 us
  Pallas kernels  174 us (94%)
  local copies, waits for them, and re-layouts  5.16 us (3%)
  other arithmetic  4.66 us (3%)
    pallas_call x1, Pallas kernels, body(): pl.pallas_call(kernel, name='outer_round', out_shape=(jax.ShapeDtypeStruc...  174 us
    unnamed x13, local copies, waits for them, and re-layouts  5.16 us
    sub x1, other arithmetic, body(): anchor_new = anchor - learn_rate * slow_new  4.66 us

profile of v5, /device:TPU:1, one launch (start us, length us, event | category | flops | bytes accessed | tf_op | source)
XLA Modules:
  0.0 184.4 jit_solution(13921949617373647044)
XLA Ops:
  0.6 0.0 copy-start
  0.6 1.2 copy-done
  1.9 0.0 copy-start.1
  1.9 1.2 copy-done.1
  3.1 0.0 copy-start.2
  3.1 0.7 copy-done.2
  3.8 0.0 copy-start.3
  3.8 0.0 copy-start.5
  3.8 173.9 %outer_round.1 = (f32[1,2,1024,512]{3,2,1,0:T(8,128)}, bf16[2,1024,512]{2,1,0:T(8,128)(2,1)S(1)}) custom-call(s32[3,1,512]{2,1,0:T(1,128)S(1)} %bitcast.1, bf16[512,1024]{1,0:T(8,128)(2,1)S(1)} %copy-done, bf16[512,1024]{1,0:T(8,128)(2,1)S(1)} %copy-done.1, f32[2,1024,512]{2,1,0:T(8,128)} %anchor.1, f32[1,2,1024,512]{3,2,1,0:T(8,128)} %momentum.1), custom_call_target="tpu_custom_call" | custom-call | tf_op jit(solution)/shard_map/outer_round/pallas_call | solution.py:628
  177.7 0.0 copy-done.3
  177.7 0.0 copy-done.5
  177.7 0.0 copy-start.4
  177.7 4.7 %multiply_subtract_fusion = (f32[2,1024,512]{2,1,0:T(8,128)}, f32[2,1024,512]{2,1,0:T(8,128)}) fusion(f32[2,1024,512]{2,1,0:T(8,128)S(1)} %copy-done.3, bf16[2,1024,512]{2,1,0:T(8,128)(2,1)S(1)} %get-tuple-element.5, f32[2,1024,512]{2,1,0:T(8,128)S(1)} %copy-done.5), kind=kLoop, calls=%fused_computation | loop fusion | flops 6291456 | bytes 18874368 | tf_op jit(solution)/shard_map/sub | solution.py:698
  182.4 0.0 copy-done.4
  182.4 2.0 %copy.10 = f32[1,2,1024,512]{3,2,1,0:T(8,128)} copy(f32[1,2,1024,512]{3,2,1,0:T(8,128)S(1)} %copy-done.4) | data formatting | bytes 8388608
Async XLA Ops:
  0.6 1.2 copy-start
  1.9 1.2 copy-start.1
  3.1 0.7 copy-start.2
  3.8 173.9 %copy-start.3 = (f32[2,1024,512]{2,1,0:T(8,128)S(1)}, f32[2,1024,512]{2,1,0:T(8,128)}, u32[]{:S(2)}) copy-start(f32[2,1024,512]{2,1,0:T(8,128)} %anchor.1) | copy-start | bytes 12582916
  3.8 174.0 %copy-start.5 = (f32[2,1024,512]{2,1,0:T(8,128)S(1)}, f32[2,1024,512]{2,1,0:T(8,128)}, u32[]{:S(2)}) copy-start(f32[2,1024,512]{2,1,0:T(8,128)} %param.11) | copy-start | bytes 12582916
  177.7 4.7 %copy-start.4 = (f32[1,2,1024,512]{3,2,1,0:T(8,128)S(1)}, f32[1,2,1024,512]{3,2,1,0:T(8,128)}, u32[]{:S(2)}) copy-start(f32[1,2,1024,512]{3,2,1,0:T(8,128)} %get-tuple-element.14) | copy-start | bytes 12582916

commit v6 on v5

--- a/solution.py
+++ b/solution.py
@@ -82,7 +82,6 @@
         first_up.wait_recv()
         mid[0] = (part[self.above, 0].astype(F32) + self.hop[0].astype(F32)).astype(BF16)
         self.start(mid.at[0], fin.at[half, 1], 4, self.first_of, 4 + half)
-        between()
         first_down.wait_recv()
         mid[1] = (part[self.below, 1].astype(F32) + self.hop[1].astype(F32)).astype(BF16)
         self.start(mid.at[1], fin.at[half, 1], 5, self.second_of, 4 + half)
@@ -150,9 +149,9 @@
 
 
 def kernel(
-    ids, tokens, targets, anchor, momentum,
+    ids_far, tokens_far, targets_far, anchor, momentum,
     moment_out, total_out,
-    weights, moment, gone, cast, out_box, in_box, twin_out, twin_in,
+    ids, tokens, targets, weights, moment, gone, cast, out_box, in_box, twin_out, twin_in,
     inputs, hidden, slope, back, want,
     near_inputs, near_hidden, near_slope, near_back, near_error, relay, carried,
     part, hop, mid, fin, give, got, error,
@@ -189,7 +188,14 @@
         pltpu.make_async_copy(anchor.at[0], weights.at[0], local.at[0]),
         pltpu.make_async_copy(anchor.at[1], weights.at[1], local.at[1]),
         pltpu.make_async_copy(momentum.at[0], moment, local.at[2]),
+        pltpu.make_async_copy(targets_far, targets, local.at[5]),
     ]
+    first_load = [
+        pltpu.make_async_copy(ids_far, ids, local.at[3]),
+        pltpu.make_async_copy(tokens_far, tokens, local.at[4]),
+    ]
+    for copy in first_load:
+        copy.start()
     for copy in load:
         copy.start()
 
@@ -330,6 +336,8 @@
         at = block_at(j)
         return remote(twin_out.at[at], twin_in.at[at], twin_send.at[j], twin_recv.at[j], twin)
 
+    for copy in first_load:
+        copy.wait()
     fetch(0)
     load[0].wait()
     load[1].wait()
@@ -354,6 +362,8 @@
             part[chunk] = out.astype(BF16).reshape(2, shard_rows, width)
 
         def idle():
+            if step == 0:
+                load[3].wait()
             want[...] = picked(step, row, targets).reshape(2, shard_rows, width)
 
         summed = ring.reduce(make, idle, drip if step == 0 else lambda: None)
@@ -411,6 +421,10 @@
         else:
             ring.pass_on()
             ring.collect(arrived)
+
+        def pass_turn(m, j):
+            turn_first(m, j).wait_recv()
+            turn_second(m, j).start()
 
         def update(m, left, right, first, last, ship):
             def one(j, carry):
@@ -461,7 +475,17 @@
             update(0, inputs, back, 0, 4, lambda j: box(0, j))
         elif step == 0:
             update(1, error.at[step], hidden, 0, 4, None)
+
+            @pl.when(jnp.logical_not(hears))
+            def _():
+                pass_turn(1, 1)
+                pass_turn(1, 3)
+
             update(0, inputs, back, 0, 4, None)
+
+            @pl.when(jnp.logical_not(hears))
+            def _():
+                pass_turn(0, 1)
         else:
             @pl.when(core == 0)
             def _():
@@ -507,30 +531,19 @@
 
             @pl.when(jnp.logical_not(hears))
             def _():
-                def pass_turn(m, j):
-                    turn_first(m, j).wait_recv()
-                    turn_second(m, j).start()
-
                 def take_turn(m, j):
                     straight(m, j).wait_recv()
                     blend(m, block_at(j), in_box[0, m, block_at(j), :].astype(F32))
 
-                pass_turn(1, 1)
                 take_turn(1, 0)
-                pass_turn(1, 3)
+                pass_turn(0, 3)
+                take_turn(1, 1)
                 take_turn(1, 2)
-                take_turn(1, 1)
-                pass_turn(0, 1)
+                take_turn(1, 3)
                 take_turn(0, 0)
-                take_turn(1, 3)
-                pass_turn(0, 3)
+                take_turn(0, 1)
                 take_turn(0, 2)
-                take_turn(0, 1)
                 take_turn(0, 3)
-                for m in (1, 0):
-                    for j in (1, 3):
-                        turn_second(m, j).wait_send()
-
             @pl.when(ships)
             def _():
                 for m in (1, 0):
@@ -538,12 +551,6 @@
                         near_m(m, j).wait_send()
                 near_shard().wait_send()
 
-            @pl.when(jnp.logical_not(ships))
-            def _():
-                for m in (1, 0):
-                    for j in range(blocks):
-                        straight(m, j).wait_send()
-
         if step == 1:
 
             def take(m, j, copy):
@@ -556,12 +563,12 @@
 
             fetch(2)
             relay_on(0, 0)
+            relay_on(0, 1)
             take(1, 2, box(1, 2))
-            relay_on(0, 1)
+            relay_on(1, 0)
             take(1, 3, box(1, 3))
-            relay_on(1, 0)
+            relay_on(1, 1)
             take(0, 0, box(0, 0))
-            relay_on(1, 1)
             take(0, 1, box(0, 1))
             take(1, 0, leg(2, 0))
             take(0, 2, box(0, 2))
@@ -572,6 +579,18 @@
             for hop_index in range(3):
                 for j in (0, 1):
                     leg(hop_index, j).wait_send()
+
+            @pl.when(jnp.logical_not(ships))
+            def _():
+                for m in (1, 0):
+                    for j in range(blocks):
+                        straight(m, j).wait_send()
+
+            @pl.when(jnp.logical_not(hears))
+            def _():
+                for m in (1, 0):
+                    for j in (1, 3):
+                        turn_second(m, j).wait_send()
 
     for step in range(INNER):
         one_step(step)
@@ -622,9 +641,10 @@
     units = anchor.shape[2]
     shard, wide = rows // 8, width // 8
     any_spec = pl.BlockSpec(memory_space=pl.ANY)
-    vmem_spec = pl.BlockSpec(memory_space=pltpu.VMEM)
+    hbm_spec = pl.BlockSpec(memory_space=pltpu.HBM)
     dma = pltpu.SemaphoreType.DMA
     ids = row_ids.reshape(INNER, 1, rows)
+    ids, tokens, targets = (pltpu.with_memory_space_constraint(x, pltpu.HBM) for x in (ids, tokens, targets))
     moment, total = pl.pallas_call(
         kernel,
         name="outer_round",
@@ -632,9 +652,12 @@
             jax.ShapeDtypeStruct(momentum.shape, F32),
             jax.ShapeDtypeStruct(anchor.shape, BF16),
         ),
-        in_specs=[vmem_spec, vmem_spec, vmem_spec, any_spec, any_spec],
+        in_specs=[hbm_spec] * 5,
         out_specs=(any_spec, any_spec),
         scratch_shapes=[
+            pltpu.VMEM((INNER, 1, rows), jnp.int32),
+            pltpu.VMEM((rows, width), BF16),
+            pltpu.VMEM((rows, width), BF16),
             pltpu.VMEM((2, width, units), F32),
             pltpu.VMEM((2, width, units), F32),
             pltpu.VMEM((2, width, units), F32),
@@ -687,10 +710,10 @@
             dma((4,)),
             dma((4,)),
             dma((4,)),
-            dma((3,)),
+            dma((6,)),
         ],
         compiler_params=pltpu.CompilerParams(
-            collective_id=0, has_side_effects=True, vmem_limit_bytes=46 * 1024 * 1024
+            collective_id=0, has_side_effects=True, vmem_limit_bytes=48 * 1024 * 1024
         ),
     )(ids, tokens, targets, anchor, momentum)
     mean = total.astype(F32) * (1.0 / lax.axis_size("replica"))

time: 186 us -> 175 us (0.941)
  Pallas kernels: 174 us -> 166 us
  local copies, waits for them, and re-layouts: 5.16 us -> 2.03 us
    pallas_call x1, Pallas kernels: 174 us -> 166 us  [body(): pl.pallas_call(kernel, name='outer_round', out_shape=(jax.ShapeDtypeStruc...]
    unnamed x13 -> x7, local copies, waits for them, and re-layouts: 5.16 us -> 2.03 us
where the time goes in v6:
time: 175 us; the launch traced here: 174 us
  Pallas kernels  166 us (95%)
  other arithmetic  4.69 us (3%)
  local copies, waits for them, and re-layouts  2.03 us (1%)
    pallas_call x1, Pallas kernels, body(): pl.pallas_call(kernel, name='outer_round', out_shape=(jax.ShapeDtypeStruc...  166 us
    sub x1, other arithmetic, body(): anchor_new = anchor - learn_rate * slow_new  4.69 us

profile of v6, /device:TPU:1, one launch (start us, length us, event | category | flops | bytes accessed | tf_op | source)
XLA Modules:
  0.0 173.9 jit_solution(7583307388225743139)
XLA Ops:
  0.6 0.0 copy-start
  0.6 0.0 copy-start.2
  0.7 166.5 %outer_round.1 = (f32[1,2,1024,512]{3,2,1,0:T(8,128)}, bf16[2,1024,512]{2,1,0:T(8,128)(2,1)S(1)}) custom-call(s32[3,1,512]{2,1,0:T(1,128)} %bitcast.1, bf16[512,1024]{1,0:T(8,128)(2,1)} %tokens_far.1, bf16[512,1024]{1,0:T(8,128)(2,1)} %targets_far.1, f32[2,1024,512]{2,1,0:T(8,128)} %anchor.1, f32[1,2,1024,512]{3,2,1,0:T(8,128)} %momentum.1), custom_call_target="tpu_custom_call" | custom-call | tf_op jit(solution)/shard_map/outer_round/pallas_call | solution.py:648
  167.1 0.0 copy-done
  167.1 0.0 copy-done.2
  167.2 0.0 copy-start.1
  167.2 4.7 %multiply_subtract_fusion = (f32[2,1024,512]{2,1,0:T(8,128)}, f32[2,1024,512]{2,1,0:T(8,128)}) fusion(f32[2,1024,512]{2,1,0:T(8,128)S(1)} %copy-done, bf16[2,1024,512]{2,1,0:T(8,128)(2,1)S(1)} %get-tuple-element.5, f32[2,1024,512]{2,1,0:T(8,128)S(1)} %copy-done.2), kind=kLoop, calls=%fused_computation | loop fusion | flops 6291456 | bytes 18874368 | tf_op jit(solution)/shard_map/sub | solution.py:721
  171.9 0.0 copy-done.1
  171.9 2.0 %copy.10 = f32[1,2,1024,512]{3,2,1,0:T(8,128)} copy(f32[1,2,1024,512]{3,2,1,0:T(8,128)S(1)} %copy-done.1) | data formatting | bytes 8388608
Async XLA Ops:
  0.6 166.5 %copy-start = (f32[2,1024,512]{2,1,0:T(8,128)S(1)}, f32[2,1024,512]{2,1,0:T(8,128)}, u32[]{:S(2)}) copy-start(f32[2,1024,512]{2,1,0:T(8,128)} %anchor.1) | copy-start | bytes 12582916
  0.6 166.5 %copy-start.2 = (f32[2,1024,512]{2,1,0:T(8,128)S(1)}, f32[2,1024,512]{2,1,0:T(8,128)}, u32[]{:S(2)}) copy-start(f32[2,1024,512]{2,1,0:T(8,128)} %param.11) | copy-start | bytes 12582916
  167.2 4.7 %copy-start.1 = (f32[1,2,1024,512]{3,2,1,0:T(8,128)S(1)}, f32[1,2,1024,512]{3,2,1,0:T(8,128)}, u32[]{:S(2)}) copy-start(f32[1,2,1024,512]{3,2,1,0:T(8,128)} %get-tuple-element.14) | copy-start | bytes 12582916

commit v7 on v6

--- a/solution.py
+++ b/solution.py
@@ -153,7 +153,7 @@
     moment_out, total_out,
     ids, tokens, targets, weights, moment, gone, cast, out_box, in_box, twin_out, twin_in,
     inputs, hidden, slope, back, want,
-    near_inputs, near_hidden, near_slope, near_back, near_error, relay, carried,
+    near_inputs, near_hidden, near_slope, near_back, near_error, relay,
     part, hop, mid, fin, give, got, error,
     part2, hop2, mid2, fin2, give2, got2, total,
     send, recv, send2, recv2, send3, recv3, box_send, box_recv, near_send, near_recv, turn_send, turn_recv,
@@ -179,9 +179,6 @@
     past = (rep + 14) % 16
     ships = (depth != 3) | (core != 1)
     hears = (depth != 0) | (core != 0)
-    turner = (low * 8 + (depth + 1) % 4 * 2 + 1 - core, ten)
-    turned = (low * 8 + (depth + 3) % 4 * 2 + 1 - core, ten)
-    beside = ((1 - low) * 8 + depth * 2 + core, ten)
     relay_start = (past // 8 * 8 + ((past // 2) % 4 + 2) % 4 * 2 + core, ten)
 
     load = [
@@ -216,7 +213,7 @@
         give, None, near_error, send3, recv3,
     )
     barrier = pltpu.get_barrier_semaphore()
-    peers = rings[0].peers() + mean_ring.peers() + [twin, relay_end, relay_start, turner, turned]
+    peers = rings[0].peers() + mean_ring.peers() + [twin, relay_end, relay_start]
     peers += [((rep + shift) % 16, ten) for shift in (1, 2, 14, 15)]
     for peer in peers:
         pl.semaphore_signal(barrier, inc=1, device_id=peer, device_id_type=MESH)
@@ -301,20 +298,6 @@
         index = m * blocks + j
         return remote(
             out_box.at[0, m, at], in_box.at[0, m, at], turn_send.at[index], turn_recv.at[index], after
-        )
-
-    def turn_first(m, j):
-        index, place = m * blocks + j, m * 2 + j // 2
-        return remote(
-            out_box.at[0, m, block_at(j)], carried.at[place],
-            turn_send.at[index], turn_recv.at[8 + place], turner,
-        )
-
-    def turn_second(m, j):
-        index, place = m * blocks + j, m * 2 + j // 2
-        return remote(
-            carried.at[place], in_box.at[0, m, block_at(j)],
-            turn_send.at[8 + place], turn_recv.at[index], beside,
         )
 
     def box(m, j):
@@ -421,10 +404,6 @@
         else:
             ring.pass_on()
             ring.collect(arrived)
-
-        def pass_turn(m, j):
-            turn_first(m, j).wait_recv()
-            turn_second(m, j).start()
 
         def update(m, left, right, first, last, ship):
             def one(j, carry):
@@ -441,14 +420,7 @@
                     @pl.when(jnp.logical_not(ships))
                     def _():
                         out_box[0, m, at, :] = kept.astype(BF16)
-
-                        @pl.when(j % 2 == 0)
-                        def _():
-                            straight(m, j).start()
-
-                        @pl.when(j % 2 == 1)
-                        def _():
-                            turn_first(m, j).start()
+                        straight(m, j).start()
 
                 if step == 1:
                     out_box[1, m, at, :] = kept.astype(BF16)
@@ -475,17 +447,7 @@
             update(0, inputs, back, 0, 4, lambda j: box(0, j))
         elif step == 0:
             update(1, error.at[step], hidden, 0, 4, None)
-
-            @pl.when(jnp.logical_not(hears))
-            def _():
-                pass_turn(1, 1)
-                pass_turn(1, 3)
-
             update(0, inputs, back, 0, 4, None)
-
-            @pl.when(jnp.logical_not(hears))
-            def _():
-                pass_turn(0, 1)
         else:
             @pl.when(core == 0)
             def _():
@@ -535,15 +497,9 @@
                     straight(m, j).wait_recv()
                     blend(m, block_at(j), in_box[0, m, block_at(j), :].astype(F32))
 
-                take_turn(1, 0)
-                pass_turn(0, 3)
-                take_turn(1, 1)
-                take_turn(1, 2)
-                take_turn(1, 3)
-                take_turn(0, 0)
-                take_turn(0, 1)
-                take_turn(0, 2)
-                take_turn(0, 3)
+                for m in (1, 0):
+                    for j in range(blocks):
+                        take_turn(m, j)
             @pl.when(ships)
             def _():
                 for m in (1, 0):
@@ -586,12 +542,6 @@
                     for j in range(blocks):
                         straight(m, j).wait_send()
 
-            @pl.when(jnp.logical_not(hears))
-            def _():
-                for m in (1, 0):
-                    for j in (1, 3):
-                        turn_second(m, j).wait_send()
-
     for step in range(INNER):
         one_step(step)
 
@@ -624,15 +574,20 @@
     ring.open()
     ring.pass_on()
     ring.collect(lambda chunk: across(core, chunk).start())
+    saves = [
+        pltpu.make_async_copy(total.at[which], total_out.at[which], local.at[place])
+        for place, which in enumerate((core, 1 - core))
+    ]
+    saves[0].start()
     for chunk in range(4):
         across(1 - core, chunk).wait_recv()
-    save = pltpu.make_async_copy(total, total_out, local.at[0])
-    save.start()
+    saves[1].start()
     for chunk in range(4):
         across(core, chunk).wait_send()
         twin_box(chunk).wait_send()
     ring.finish()
-    save.wait()
+    for save in saves:
+        save.wait()
     store.wait()
 
 
@@ -677,7 +632,6 @@
             pltpu.VMEM((rows, units), BF16),
             pltpu.VMEM((rows, width), BF16),
             pltpu.VMEM((2, 2, width // 4, units), BF16),
-            pltpu.VMEM((4, width // 4, units), BF16),
             pltpu.VMEM((4, 2, shard, width), BF16),
             pltpu.VMEM((INNER, 2, shard, width), BF16),
             pltpu.VMEM((2, shard, width), BF16),
@@ -702,8 +656,8 @@
             dma((8,)),
             dma((13,)),
             dma((13,)),
-            dma((12,)),
-            dma((12,)),
+            dma((8,)),
+            dma((8,)),
             dma((3, 2)),
             dma((3, 2)),
             dma((4,)),

time: 175 us -> 183 us (1.046)
  Pallas kernels: 166 us -> 174 us
    pallas_call x1, Pallas kernels: 166 us -> 174 us  [body(): pl.pallas_call(kernel, name='outer_round', out_shape=(jax.ShapeDtypeStruc...]
where the time goes in v7:
time: 183 us; the launch traced here: 182 us
  Pallas kernels  174 us (95%)
  other arithmetic  4.69 us (3%)
  local copies, waits for them, and re-layouts  2.03 us (1%)
    pallas_call x1, Pallas kernels, body(): pl.pallas_call(kernel, name='outer_round', out_shape=(jax.ShapeDtypeStruc...  174 us
    sub x1, other arithmetic, body(): anchor_new = anchor - learn_rate * slow_new  4.69 us

profile of v7, /device:TPU:1, one launch (start us, length us, event | category | flops | bytes accessed | tf_op | source)
XLA Modules:
  0.0 181.6 jit_solution(7883546969683460336)
XLA Ops:
  0.6 0.0 copy-start
  0.6 0.0 copy-start.2
  0.7 174.2 %outer_round.1 = (f32[1,2,1024,512]{3,2,1,0:T(8,128)}, bf16[2,1024,512]{2,1,0:T(8,128)(2,1)S(1)}) custom-call(s32[3,1,512]{2,1,0:T(1,128)} %bitcast.1, bf16[512,1024]{1,0:T(8,128)(2,1)} %tokens_far.1, bf16[512,1024]{1,0:T(8,128)(2,1)} %targets_far.1, f32[2,1024,512]{2,1,0:T(8,128)} %anchor.1, f32[1,2,1024,512]{3,2,1,0:T(8,128)} %momentum.1), custom_call_target="tpu_custom_call" | custom-call | tf_op jit(solution)/shard_map/outer_round/pallas_call | solution.py:603
  174.8 0.0 copy-done
  174.9 0.0 copy-done.2
  174.9 0.0 copy-start.1
  174.9 4.7 %multiply_subtract_fusion = (f32[2,1024,512]{2,1,0:T(8,128)}, f32[2,1024,512]{2,1,0:T(8,128)}) fusion(f32[2,1024,512]{2,1,0:T(8,128)S(1)} %copy-done, bf16[2,1024,512]{2,1,0:T(8,128)(2,1)S(1)} %get-tuple-element.5, f32[2,1024,512]{2,1,0:T(8,128)S(1)} %copy-done.2), kind=kLoop, calls=%fused_computation | loop fusion | flops 6291456 | bytes 18874368 | tf_op jit(solution)/shard_map/sub | solution.py:675
  179.6 0.0 copy-done.1
  179.6 2.0 %copy.10 = f32[1,2,1024,512]{3,2,1,0:T(8,128)} copy(f32[1,2,1024,512]{3,2,1,0:T(8,128)S(1)} %copy-done.1) | data formatting | bytes 8388608
Async XLA Ops:
  0.6 174.2 %copy-start = (f32[2,1024,512]{2,1,0:T(8,128)S(1)}, f32[2,1024,512]{2,1,0:T(8,128)}, u32[]{:S(2)}) copy-start(f32[2,1024,512]{2,1,0:T(8,128)} %anchor.1) | copy-start | bytes 12582916
  0.6 174.2 %copy-start.2 = (f32[2,1024,512]{2,1,0:T(8,128)S(1)}, f32[2,1024,512]{2,1,0:T(8,128)}, u32[]{:S(2)}) copy-start(f32[2,1024,512]{2,1,0:T(8,128)} %param.11) | copy-start | bytes 12582916
  174.9 4.7 %copy-start.1 = (f32[1,2,1024,512]{3,2,1,0:T(8,128)S(1)}, f32[1,2,1024,512]{3,2,1,0:T(8,128)}, u32[]{:S(2)}) copy-start(f32[1,2,1024,512]{3,2,1,0:T(8,128)} %get-tuple-element.14) | copy-start | bytes 12582916

commit v8 on v6

--- a/solution.py
+++ b/solution.py
@@ -296,25 +296,18 @@
             lax.fori_loop(0, tall // 64, decay, 0)
             near_m(m, j).start()
 
-    def straight(m, j):
-        at = block_at(j)
-        index = m * blocks + j
-        return remote(
-            out_box.at[0, m, at], in_box.at[0, m, at], turn_send.at[index], turn_recv.at[index], after
-        )
-
     def turn_first(m, j):
-        index, place = m * blocks + j, m * 2 + j // 2
+        place = m * blocks + j
         return remote(
             out_box.at[0, m, block_at(j)], carried.at[place],
-            turn_send.at[index], turn_recv.at[8 + place], turner,
+            turn_send.at[place], turn_recv.at[8 + place], turner,
         )
 
     def turn_second(m, j):
-        index, place = m * blocks + j, m * 2 + j // 2
+        place = m * blocks + j
         return remote(
             carried.at[place], in_box.at[0, m, block_at(j)],
-            turn_send.at[8 + place], turn_recv.at[index], beside,
+            turn_send.at[8 + place], turn_recv.at[place], beside,
         )
 
     def box(m, j):
@@ -441,14 +434,7 @@
                     @pl.when(jnp.logical_not(ships))
                     def _():
                         out_box[0, m, at, :] = kept.astype(BF16)
-
-                        @pl.when(j % 2 == 0)
-                        def _():
-                            straight(m, j).start()
-
-                        @pl.when(j % 2 == 1)
-                        def _():
-                            turn_first(m, j).start()
+                        turn_first(m, j).start()
 
                 if step == 1:
                     out_box[1, m, at, :] = kept.astype(BF16)
@@ -478,14 +464,15 @@
 
             @pl.when(jnp.logical_not(hears))
             def _():
+                pass_turn(1, 0)
                 pass_turn(1, 1)
+
+            update(0, inputs, back, 0, 4, None)
+
+            @pl.when(jnp.logical_not(hears))
+            def _():
+                pass_turn(1, 2)
                 pass_turn(1, 3)
-
-            update(0, inputs, back, 0, 4, None)
-
-            @pl.when(jnp.logical_not(hears))
-            def _():
-                pass_turn(0, 1)
         else:
             @pl.when(core == 0)
             def _():
@@ -532,18 +519,19 @@
             @pl.when(jnp.logical_not(hears))
             def _():
                 def take_turn(m, j):
-                    straight(m, j).wait_recv()
+                    turn_second(m, j).wait_recv()
                     blend(m, block_at(j), in_box[0, m, block_at(j), :].astype(F32))
 
+                pass_turn(0, 0)
+                pass_turn(0, 1)
                 take_turn(1, 0)
+                pass_turn(0, 2)
+                take_turn(1, 1)
                 pass_turn(0, 3)
-                take_turn(1, 1)
                 take_turn(1, 2)
                 take_turn(1, 3)
-                take_turn(0, 0)
-                take_turn(0, 1)
-                take_turn(0, 2)
-                take_turn(0, 3)
+                for j in range(blocks):
+                    take_turn(0, j)
             @pl.when(ships)
             def _():
                 for m in (1, 0):
@@ -584,12 +572,12 @@
             def _():
                 for m in (1, 0):
                     for j in range(blocks):
-                        straight(m, j).wait_send()
+                        turn_first(m, j).wait_send()
 
             @pl.when(jnp.logical_not(hears))
             def _():
                 for m in (1, 0):
-                    for j in (1, 3):
+                    for j in range(blocks):
                         turn_second(m, j).wait_send()
 
     for step in range(INNER):
@@ -624,15 +612,20 @@
     ring.open()
     ring.pass_on()
     ring.collect(lambda chunk: across(core, chunk).start())
+    saves = [
+        pltpu.make_async_copy(total.at[which], total_out.at[which], local.at[place])
+        for place, which in enumerate((core, 1 - core))
+    ]
+    saves[0].start()
     for chunk in range(4):
         across(1 - core, chunk).wait_recv()
-    save = pltpu.make_async_copy(total, total_out, local.at[0])
-    save.start()
+    saves[1].start()
     for chunk in range(4):
         across(core, chunk).wait_send()
         twin_box(chunk).wait_send()
     ring.finish()
-    save.wait()
+    for save in saves:
+        save.wait()
     store.wait()
 
 
@@ -677,7 +670,7 @@
             pltpu.VMEM((rows, units), BF16),
             pltpu.VMEM((rows, width), BF16),
             pltpu.VMEM((2, 2, width // 4, units), BF16),
-            pltpu.VMEM((4, width // 4, units), BF16),
+            pltpu.VMEM((8, width // 4, units), BF16),
             pltpu.VMEM((4, 2, shard, width), BF16),
             pltpu.VMEM((INNER, 2, shard, width), BF16),
             pltpu.VMEM((2, shard, width), BF16),
@@ -702,8 +695,8 @@
             dma((8,)),
             dma((13,)),
             dma((13,)),
-            dma((12,)),
-            dma((12,)),
+            dma((16,)),
+            dma((16,)),
             dma((3, 2)),
             dma((3, 2)),
             dma((4,)),
@@ -713,7 +706,7 @@
             dma((6,)),
         ],
         compiler_params=pltpu.CompilerParams(
-            collective_id=0, has_side_effects=True, vmem_limit_bytes=48 * 1024 * 1024
+            collective_id=0, has_side_effects=True, vmem_limit_bytes=49 * 1024 * 1024
         ),
     )(ids, tokens, targets, anchor, momentum)
     mean = total.astype(F32) * (1.0 / lax.axis_size("replica"))

time: 175 us -> 177 us (1.011)
  Pallas kernels: 166 us -> 169 us
    pallas_call x1, Pallas kernels: 166 us -> 169 us  [body(): pl.pallas_call(kernel, name='outer_round', out_shape=(jax.ShapeDtypeStruc...]
where the time goes in v8:
time: 177 us
  Pallas kernels  169 us (95%)
  other arithmetic  4.69 us (3%)
  local copies, waits for them, and re-layouts  2.03 us (1%)
    pallas_call x1, Pallas kernels, body(): pl.pallas_call(kernel, name='outer_round', out_shape=(jax.ShapeDtypeStruc...  169 us
    sub x1, other arithmetic, body(): anchor_new = anchor - learn_rate * slow_new  4.69 us

profile of v8, /device:TPU:1, one launch (start us, length us, event | category | flops | bytes accessed | tf_op | source)
XLA Modules:
  0.0 176.6 jit_solution(5081878258653431528)
XLA Ops:
  0.6 0.0 copy-start
  0.6 0.0 copy-start.2
  0.7 169.2 %outer_round.1 = (f32[1,2,1024,512]{3,2,1,0:T(8,128)}, bf16[2,1024,512]{2,1,0:T(8,128)(2,1)S(1)}) custom-call(s32[3,1,512]{2,1,0:T(1,128)} %bitcast.1, bf16[512,1024]{1,0:T(8,128)(2,1)} %tokens_far.1, bf16[512,1024]{1,0:T(8,128)(2,1)} %targets_far.1, f32[2,1024,512]{2,1,0:T(8,128)} %anchor.1, f32[1,2,1024,512]{3,2,1,0:T(8,128)} %momentum.1), custom_call_target="tpu_custom_call" | custom-call | tf_op jit(solution)/shard_map/outer_round/pallas_call | solution.py:641
  169.8 0.0 copy-done
  169.9 0.0 copy-done.2
  169.9 0.0 copy-start.1
  169.9 4.7 %multiply_subtract_fusion = (f32[2,1024,512]{2,1,0:T(8,128)}, f32[2,1024,512]{2,1,0:T(8,128)}) fusion(f32[2,1024,512]{2,1,0:T(8,128)S(1)} %copy-done, bf16[2,1024,512]{2,1,0:T(8,128)(2,1)S(1)} %get-tuple-element.5, f32[2,1024,512]{2,1,0:T(8,128)S(1)} %copy-done.2), kind=kLoop, calls=%fused_computation | loop fusion | flops 6291456 | bytes 18874368 | tf_op jit(solution)/shard_map/sub | solution.py:714
  174.6 0.0 copy-done.1
  174.6 2.0 %copy.10 = f32[1,2,1024,512]{3,2,1,0:T(8,128)} copy(f32[1,2,1024,512]{3,2,1,0:T(8,128)S(1)} %copy-done.1) | data formatting | bytes 8388608
Async XLA Ops:
  0.6 169.2 %copy-start = (f32[2,1024,512]{2,1,0:T(8,128)S(1)}, f32[2,1024,512]{2,1,0:T(8,128)}, u32[]{:S(2)}) copy-start(f32[2,1024,512]{2,1,0:T(8,128)} %anchor.1) | copy-start | bytes 12582916
  0.6 169.2 %copy-start.2 = (f32[2,1024,512]{2,1,0:T(8,128)S(1)}, f32[2,1024,512]{2,1,0:T(8,128)}, u32[]{:S(2)}) copy-start(f32[2,1024,512]{2,1,0:T(8,128)} %param.11) | copy-start | bytes 12582916
  169.9 4.7 %copy-start.1 = (f32[1,2,1024,512]{3,2,1,0:T(8,128)S(1)}, f32[1,2,1024,512]{3,2,1,0:T(8,128)}, u32[]{:S(2)}) copy-start(f32[1,2,1024,512]{3,2,1,0:T(8,128)} %get-tuple-element.14) | copy-start | bytes 12582916

commit v9 on v8

--- a/solution.py
+++ b/solution.py
@@ -303,6 +303,12 @@
             turn_send.at[place], turn_recv.at[8 + place], turner,
         )
 
+    def straight(m, j):
+        at, place = block_at(j), m * blocks + j
+        return remote(
+            out_box.at[0, m, at], in_box.at[0, m, at], turn_send.at[place], turn_recv.at[place], after
+        )
+
     def turn_second(m, j):
         place = m * blocks + j
         return remote(
@@ -434,7 +440,17 @@
                     @pl.when(jnp.logical_not(ships))
                     def _():
                         out_box[0, m, at, :] = kept.astype(BF16)
-                        turn_first(m, j).start()
+                        if m == 1:
+                            turn_first(m, j).start()
+                        else:
+
+                            @pl.when(j < 2)
+                            def _():
+                                turn_first(m, j).start()
+
+                            @pl.when(j >= 2)
+                            def _():
+                                straight(m, j).start()
 
                 if step == 1:
                     out_box[1, m, at, :] = kept.astype(BF16)
@@ -525,9 +541,7 @@
                 pass_turn(0, 0)
                 pass_turn(0, 1)
                 take_turn(1, 0)
-                pass_turn(0, 2)
                 take_turn(1, 1)
-                pass_turn(0, 3)
                 take_turn(1, 2)
                 take_turn(1, 3)
                 for j in range(blocks):
@@ -577,7 +591,7 @@
             @pl.when(jnp.logical_not(hears))
             def _():
                 for m in (1, 0):
-                    for j in range(blocks):
+                    for j in range(blocks if m == 1 else 2):
                         turn_second(m, j).wait_send()
 
     for step in range(INNER):

time: 177 us -> 180 us (1.017)
  Pallas kernels: 169 us -> 172 us
    pallas_call x1, Pallas kernels: 169 us -> 172 us  [body(): pl.pallas_call(kernel, name='outer_round', out_shape=(jax.ShapeDtypeStruc...]
where the time goes in v9:
time: 180 us
  Pallas kernels  172 us (96%)
  other arithmetic  4.69 us (3%)
  local copies, waits for them, and re-layouts  2.03 us (1%)
    pallas_call x1, Pallas kernels, body(): pl.pallas_call(kernel, name='outer_round', out_shape=(jax.ShapeDtypeStruc...  172 us
    sub x1, other arithmetic, body(): anchor_new = anchor - learn_rate * slow_new  4.69 us

profile of v9, /device:TPU:1, one launch (start us, length us, event | category | flops | bytes accessed | tf_op | source)
XLA Modules:
  0.0 179.7 jit_solution(3508234495653539712)
XLA Ops:
  0.6 0.0 copy-start
  0.6 0.0 copy-start.2
  0.7 172.3 %outer_round.1 = (f32[1,2,1024,512]{3,2,1,0:T(8,128)}, bf16[2,1024,512]{2,1,0:T(8,128)(2,1)S(1)}) custom-call(s32[3,1,512]{2,1,0:T(1,128)} %bitcast.1, bf16[512,1024]{1,0:T(8,128)(2,1)} %tokens_far.1, bf16[512,1024]{1,0:T(8,128)(2,1)} %targets_far.1, f32[2,1024,512]{2,1,0:T(8,128)} %anchor.1, f32[1,2,1024,512]{3,2,1,0:T(8,128)} %momentum.1), custom_call_target="tpu_custom_call" | custom-call | tf_op jit(solution)/shard_map/outer_round/pallas_call | solution.py:655
  173.0 0.0 copy-done
  173.0 0.0 copy-done.2
  173.0 0.0 copy-start.1
  173.0 4.7 %multiply_subtract_fusion = (f32[2,1024,512]{2,1,0:T(8,128)}, f32[2,1024,512]{2,1,0:T(8,128)}) fusion(f32[2,1024,512]{2,1,0:T(8,128)S(1)} %copy-done, bf16[2,1024,512]{2,1,0:T(8,128)(2,1)S(1)} %get-tuple-element.5, f32[2,1024,512]{2,1,0:T(8,128)S(1)} %copy-done.2), kind=kLoop, calls=%fused_computation | loop fusion | flops 6291456 | bytes 18874368 | tf_op jit(solution)/shard_map/sub | solution.py:728
  177.7 0.0 copy-done.1
  177.7 2.0 %copy.10 = f32[1,2,1024,512]{3,2,1,0:T(8,128)} copy(f32[1,2,1024,512]{3,2,1,0:T(8,128)S(1)} %copy-done.1) | data formatting | bytes 8388608
Async XLA Ops:
  0.6 172.4 %copy-start = (f32[2,1024,512]{2,1,0:T(8,128)S(1)}, f32[2,1024,512]{2,1,0:T(8,128)}, u32[]{:S(2)}) copy-start(f32[2,1024,512]{2,1,0:T(8,128)} %anchor.1) | copy-start | bytes 12582916
  0.6 172.4 %copy-start.2 = (f32[2,1024,512]{2,1,0:T(8,128)S(1)}, f32[2,1024,512]{2,1,0:T(8,128)}, u32[]{:S(2)}) copy-start(f32[2,1024,512]{2,1,0:T(8,128)} %param.11) | copy-start | bytes 12582916
  173.0 4.7 %copy-start.1 = (f32[1,2,1024,512]{3,2,1,0:T(8,128)S(1)}, f32[1,2,1024,512]{3,2,1,0:T(8,128)}, u32[]{:S(2)}) copy-start(f32[1,2,1024,512]{3,2,1,0:T(8,128)} %get-tuple-element.14) | copy-start | bytes 12582916
